TPU v7x, 256 devices: a whole 4x4x8 slice. The times are simulated.
256 devices in a mesh: lon: 32 (over z, x_hi, core), lat: 8 (over y, x_lo).
Axes of the slice: x: 4 (x_hi: 2, x_lo: 2; x = x_hi * 2 + x_lo), y: 4, z: 8, core: 2. Of those that a mesh axis runs over, the one named last changes fastest.
Arguments:
- field: bfloat16 [32, 1024, 256], P('lat', 'lon'), may hold values from -6 to 6
- cotangent: bfloat16 [32, 1024, 256], P('lat', 'lon'), may hold values from -6 to 6
- mix_weight: bfloat16 [256, 256], replicated, may hold values from -0.375 to 0.375
- first_weight: float32 [3, 256], replicated, may hold values from -0.34 to 0.34
- first_bias: float32 [256], replicated, may hold values from -0.5 to 0.5
- hidden_weight: bfloat16 [256, 256], replicated, may hold values from -0.375 to 0.375
- hidden_bias: float32 [256], replicated, may hold values from -1 to 1
- output_weight: bfloat16 [256, 256], replicated, may hold values from -0.375 to 0.375
- output_bias: float32 [256], replicated, may hold values from -0.5 to 0.5
- lon_half: int32 [32], replicated, may hold values from 3 to 32, as said below
- lat_half: int32 [32], replicated, may hold values from 1 to 4, as said below
Outputs:
- grad_field: bfloat16 [32, 1024, 256], P('lat', 'lon')
- grad_mix: float32 [256, 256], replicated
- grad_first_weight: float32 [3, 256], replicated
- grad_first_bias: float32 [256], replicated
- grad_hidden_weight: float32 [256, 256], replicated
- grad_hidden_bias: float32 [256], replicated
- grad_output_weight: float32 [256, 256], replicated
- grad_output_bias: float32 [256], replicated
Inputs may be any that keep to these rules, and one draw needn't show every extreme that they name: lon_half[i] is row i's half-width in longitude: 32 in the first and last rows. lat_half[i] is row i's half-width in latitude: 4 in the first and last rows.
All inputs are finite; a program needn't handle non-finite values.
Results may differ from a plain program's by a relative error of at most 0.0064.
Values may be sent and summed in bfloat16 or wider, within the bound.
No kernel may reach another device: no remote copies, remote signals or barrier semaphores. Data moves between devices by JAX's collectives and lax.ppermute only.
A program may use at most 128 MiB of HBM per device.

v0:
```python
import math

import jax
import jax.numpy as jnp
from jax import lax
from jax.sharding import PartitionSpec as P

HLON = 32
HLAT = 4


first_omega = 30.0


def extended(block, sides, width, periodic):
    for axis, dim in sides:
        count = lax.axis_size(axis)
        forward = [(i, i + 1) for i in range(count - 1)]
        if periodic:
            forward.append((count - 1, 0))
        backward = [(target, source) for source, target in forward]
        low = lax.ppermute(
            lax.slice_in_dim(block, block.shape[dim] - width, None, axis=dim), axis, forward
        )
        high = lax.ppermute(lax.slice_in_dim(block, 0, width, axis=dim), axis, backward)
        block = jnp.concatenate([low, block, high], axis=dim)
    return block


def inner_rows(left, right):
    return lax.dot_general(
        left,
        right,
        (((0,), (0,)), ((), ())),
        precision=lax.Precision.HIGHEST,
        preferred_element_type=jnp.float32,
    )


def tap_kernels(first_row, half_lon, half_lat, grid_rows, weights):
    first_weight, first_bias, hidden_weight, hidden_bias, output_weight, output_bias = weights
    row_count = half_lon.shape[0]
    taps_lon = 2 * HLON + 4
    taps_lat = 2 * HLAT + 1
    shape = (row_count, taps_lon, taps_lat)
    row_index = (first_row + jnp.arange(row_count)).astype(jnp.float32)
    shift_lon = jnp.arange(taps_lon) - HLON
    shift_lat = jnp.arange(taps_lat) - HLAT
    wide_lon = half_lon[:, None, None]
    wide_lat = half_lat[:, None, None]
    lon_coord = jnp.broadcast_to(
        shift_lon[None, :, None].astype(jnp.float32) / wide_lon.astype(jnp.float32), shape
    )
    lat_coord = jnp.broadcast_to(
        shift_lat[None, None, :].astype(jnp.float32) / wide_lat.astype(jnp.float32), shape
    )
    lat_sine = jnp.broadcast_to(
        jnp.sin(jnp.pi * ((row_index + 0.5) / grid_rows - 0.5))[:, None, None], shape
    )
    inside = (jnp.abs(shift_lon)[None, :, None] <= wide_lon) & (
        jnp.abs(shift_lat)[None, None, :] <= wide_lat
    )
    row_norm = lax.rsqrt(((2 * half_lon + 1) * (2 * half_lat + 1)).astype(jnp.float32))
    tap_scale = jnp.where(
        inside, jnp.broadcast_to(row_norm[:, None, None], shape), jnp.zeros(shape, jnp.float32)
    )
    pre_first = (
        lon_coord[..., None] * first_weight[0]
        + lat_coord[..., None] * first_weight[1]
        + lat_sine[..., None] * first_weight[2]
        + first_bias
    )
    pre_first = pre_first.reshape(-1, first_weight.shape[1])
    hidden_first = jnp.sin(first_omega * pre_first).astype(jnp.bfloat16)
    pre_hidden = (
        jnp.dot(hidden_first, hidden_weight, preferred_element_type=jnp.float32) + hidden_bias
    )
    hidden_second = jnp.sin(pre_hidden).astype(jnp.bfloat16)
    raw_kernel = (
        jnp.dot(hidden_second, output_weight, preferred_element_type=jnp.float32) + output_bias
    )
    kernel = (raw_kernel.reshape(row_count, taps_lon, taps_lat, -1) * tap_scale[..., None]).astype(
        jnp.bfloat16
    )
    features = jnp.stack(
        (lon_coord.reshape(-1), lat_coord.reshape(-1), lat_sine.reshape(-1)), axis=0
    )
    return (
        kernel,
        (features, tap_scale.reshape(-1), pre_first, hidden_first, pre_hidden, hidden_second),
    )


def forward_pass(field_pad, mixed_cot, kernel_own, widths_own):
    lat_rows, lon_cols, channels = mixed_cot.shape
    taps_lat = kernel_own.shape[2]
    widest = jnp.max(widths_own)
    group_count = (2 * widest + 4) // 4

    def forward_one_group(group, carry):
        total, gradients = carry
        first_tap = HLON - widest + 4 * group
        kern_block = lax.dynamic_slice_in_dim(kernel_own, first_tap, 4, 1)
        band_cols = lax.dynamic_slice_in_dim(field_pad, first_tap + 4, lon_cols + 3, 1)
        pieces = []
        for t in range(4):
            shifted = band_cols[:, t : t + lon_cols]
            per_row = []
            for a in range(taps_lat):
                source = shifted[a : a + lat_rows].astype(jnp.float32)
                total = total + source * kern_block[:, t, a][:, None, :].astype(jnp.float32)
                per_row.append(jnp.sum(source * mixed_cot.astype(jnp.float32), axis=1))
            pieces.append(jnp.stack(per_row, axis=1))
        gradients = lax.dynamic_update_slice_in_dim(
            gradients, jnp.stack(pieces, axis=1), first_tap, 1
        )
        return (total, gradients)

    start_total = jnp.zeros((lat_rows, lon_cols, channels), jnp.float32)
    start_grads = jnp.zeros(kernel_own.shape, jnp.float32)
    return lax.fori_loop(0, group_count, forward_one_group, (start_total, start_grads))


def backward_pass(cot_pad, kernel_ext, widths_ext, lat_rows, lon_cols):
    taps_lat = kernel_ext.shape[2]
    channels = kernel_ext.shape[3]
    widest = jnp.max(widths_ext)
    group_count = (2 * widest + 4) // 4

    def backward_one_group(group, total):
        first_tap = HLON - widest + 4 * group
        kern_block = lax.dynamic_slice_in_dim(kernel_ext, first_tap, 4, 1)
        begin_col = 2 * HLON + 4 - (first_tap + 3)
        band_cols = lax.dynamic_slice_in_dim(cot_pad, begin_col, lon_cols + 3, 1)
        for t in range(4):
            shifted = band_cols[:, 3 - t : 3 - t + lon_cols]
            for a in range(taps_lat):
                row_from = 2 * HLAT - a
                total = total + shifted[row_from : row_from + lat_rows].astype(
                    jnp.float32
                ) * kern_block[row_from : row_from + lat_rows, t, a][:, None, :].astype(jnp.float32)
        return total

    start_total = jnp.zeros((lat_rows, lon_cols, channels), jnp.float32)
    return lax.fori_loop(0, group_count, backward_one_group, start_total)


def siren_backward(grad_kernel, saved, weights):
    first_weight, first_bias, hidden_weight, hidden_bias, output_weight, output_bias = weights
    features, tap_scale, pre_first, hidden_first, pre_hidden, hidden_second = saved
    highest = lax.Precision.HIGHEST
    grad_raw = grad_kernel.reshape(tap_scale.shape[0], -1) * tap_scale[:, None]
    part_output_weight = inner_rows(hidden_second.astype(jnp.float32), grad_raw)
    grad_output_bias = jnp.sum(grad_raw, axis=0)
    grad_hidden_out = lax.dot_general(
        grad_raw,
        output_weight.astype(jnp.float32),
        (((1,), (1,)), ((), ())),
        precision=highest,
        preferred_element_type=jnp.float32,
    )
    grad_pre_hidden = grad_hidden_out * jnp.cos(pre_hidden)
    grad_hidden_weight = inner_rows(hidden_first.astype(jnp.float32), grad_pre_hidden)
    grad_hidden_bias = jnp.sum(grad_pre_hidden, axis=0)
    grad_first_out = lax.dot_general(
        grad_pre_hidden,
        hidden_weight.astype(jnp.float32),
        (((1,), (1,)), ((), ())),
        precision=highest,
        preferred_element_type=jnp.float32,
    )
    grad_pre_first = first_omega * grad_first_out * jnp.cos(first_omega * pre_first)
    grad_first_weight = jnp.dot(features, grad_pre_first, precision=highest)
    grad_first_bias = jnp.sum(grad_pre_first, axis=0)
    return (
        grad_first_weight,
        grad_first_bias,
        grad_hidden_weight,
        grad_hidden_bias,
        part_output_weight,
        grad_output_bias,
    )


def shards(
    field,
    cotangent,
    mix_weight,
    first_weight,
    first_bias,
    hidden_weight,
    hidden_bias,
    output_weight,
    output_bias,
    lon_half,
    lat_half,
):
    lat_rows, lon_cols, channels = field.shape
    grid_rows = lat_rows * lax.axis_size("lat")
    grid_cols = lon_cols * lax.axis_size("lon")
    row_start = lax.axis_index("lat") * lat_rows
    weights = (first_weight, first_bias, hidden_weight, hidden_bias, output_weight, output_bias)
    flat_cot = cotangent.reshape(-1, channels)
    mixed_cot = lax.dot_general(
        flat_cot, mix_weight, (((1,), (1,)), ((), ())), preferred_element_type=jnp.float32
    ).astype(jnp.bfloat16)
    mixed_cot = mixed_cot.reshape(lat_rows, lon_cols, channels)
    stacked = jnp.stack((field, mixed_cot), axis=2)
    with_rows = extended(stacked, (("lat", 0),), HLAT, False)
    own_lon = lax.dynamic_slice_in_dim(lon_half, row_start, lat_rows)
    edge_lon = lax.dynamic_slice_in_dim(
        jnp.pad(lon_half, HLAT, mode="edge"), row_start, lat_rows + 2 * HLAT
    )
    edge_lat = lax.dynamic_slice_in_dim(
        jnp.pad(lat_half, HLAT, mode="edge"), row_start, lat_rows + 2 * HLAT
    )
    tap_points = (2 * HLON + 4) * (2 * HLAT + 1)
    kernel_ext, saved_ext = tap_kernels(row_start - HLAT, edge_lon, edge_lat, grid_rows, weights)
    kernel_own = kernel_ext[HLAT : HLAT + lat_rows]
    first_point = HLAT * tap_points
    finish = first_point + lat_rows * tap_points
    saved = (
        saved_ext[0][:, first_point:finish],
        saved_ext[1][first_point:finish],
        saved_ext[2][first_point:finish],
        saved_ext[3][first_point:finish],
        saved_ext[4][first_point:finish],
        saved_ext[5][first_point:finish],
    )
    with_cols = extended(with_rows, (("lon", 1),), HLON, True)
    padded = jnp.pad(with_cols, ((0, 0), (4, 4), (0, 0), (0, 0)))
    field_pad = padded[:, :, 0]
    cot_pad = padded[:, :, 1]
    conv_total, grad_kernel = forward_pass(field_pad, mixed_cot, kernel_own, own_lon)
    back_total = backward_pass(cot_pad, kernel_ext, edge_lon, lat_rows, lon_cols)
    conv_out = conv_total.astype(jnp.bfloat16)
    grad_field = back_total.astype(jnp.bfloat16)
    grad_mix = lax.dot_general(
        conv_out.reshape(-1, channels),
        flat_cot,
        (((0,), (0,)), ((), ())),
        preferred_element_type=jnp.float32,
    )
    gradients = siren_backward(grad_kernel, saved, weights)
    inverse = 1.0 / math.sqrt(grid_rows * grid_cols)
    summed = lax.psum(
        (
            grad_mix * inverse,
            gradients[0] * inverse,
            gradients[1] * inverse,
            gradients[2] * inverse,
            gradients[3] * inverse,
            gradients[4] * inverse,
            gradients[5] * inverse,
        ),
        ("lon", "lat"),
    )
    return (grad_field, summed[0], summed[1], summed[2], summed[3], summed[4], summed[5], summed[6])


def solution(mesh):
    in_specs = (
        P("lat", "lon", None),
        P("lat", "lon", None),
        P(),
        P(),
        P(),
        P(),
        P(),
        P(),
        P(),
        P(),
        P(),
    )
    out_specs = (P("lat", "lon", None), P(), P(), P(), P(), P(), P(), P())
    return jax.shard_map(shards, mesh=mesh, in_specs=in_specs, out_specs=out_specs, check_vma=False)
```

profile of v0, /device:TPU:1, one launch (start us, length us, event | category | flops | bytes accessed | tf_op | source)
XLA Modules:
  0.0 622.7 jit_solution(2367591374362019713)
XLA Ops:
  9.3 3.9 collective-permute-start
  23.5 29.9 %sine_convert_fusion.1 = bf16[7344,256]{1,0:T(8,128)(2,1)} fusion(f32[256]{0:T(256)} %param.19, f32[256]{0:T(256)S(1)} %bitcast.422, f32[7344]{0:T(1024)S(1)} %mul_broadcast_in_dim_broadcast_in_dim.40, f32[256]{0:T(256)S(1)} %bitcast.425, f32[7344]{0:T(1024)S(1)} %mul_broadcast_in_dim_broadcast_in_dim.37, f32[256]{0:T(256)S(1)} %bitcast.419, ...), kind=kLoop, calls=%fused_computation.366 | loop fusion | flops 15040512 | bytes 3852352 | tf_op jit(solution)/shard_map/convert_element_type | solution.py:74
  53.4 52.7 %sine_convert_fusion = (bf16[7344,256]{1,0:T(8,128)(2,1)S(1)}, f32[7344,256]{1,0:T(8,128)}) fusion(f32[256]{0:T(256)S(1)} %copy-done.11, bf16[256,256]{1,0:T(8,128)(2,1)S(1)} %copy-done, f32[256]{0:T(256)S(1)} %copy-done.9, f32[256]{0:T(256)S(1)} %bitcast.423, f32[7344]{0:T(1024)S(1)} %mul_broadcast_in_dim_broadcast_in_dim.40, f32[256]{0:T(256)S(1)} %bitcast.426, ...), kind=kOutput, calls=%fused_computation.365 | convolution fusion | flops 981393408 | bytes 11504704 | tf_op jit(solution)/shard_map/dot_general | solution.py:76
  106.1 1.8 copy-done.2
  107.9 4.2 convolution_add_fusion
  112.1 10.4 %reshape.1109 = f32[12,68,9,256]{3,2,1,0:T(8,128)} reshape(f32[7344,256]{1,0:T(8,128)} %convolution_add_fusion) | data formatting | bytes 15040512 | tf_op jit(solution)/shard_map/reshape | solution.py:82
  123.7 3.3 collective-permute-start.2
  127.0 8.3 %multiply_convert_fusion = bf16[12,68,9,256]{3,2,1,0:T(8,128)(2,1)} fusion(f32[12,68,9,256]{3,2,1,0:T(8,128)} %reshape.1109, f32[12,68,9]{2,1,0:T(8,128)S(1)} %and_select_fusion), kind=kLoop, calls=%fused_computation.362 | loop fusion | flops 3760128 | bytes 11309760 | tf_op jit(solution)/shard_map/convert_element_type | solution.py:82
  140.7 9.4 %copy.21 = bf16[12,68,9,256]{3,0,2,1:T(8,128)(2,1)} copy(bf16[12,68,9,256]{3,2,1,0:T(8,128)(2,1)} %multiply_convert_fusion) | data formatting | bytes 7520256 | tf_op jit(solution)/shard_map/while | solution.py:145
  150.8 2.7 copy.22
  154.3 17.0 %multiply_cosine_fusion = f32[4,68,9,256]{3,2,1,0:T(8,128)} fusion(f32[256]{0:T(256)S(1)} %copy-done.9, f32[256]{0:T(256)S(1)} %bitcast.424, f32[4]{0:T(128)S(1)} %slice.1031, f32[256]{0:T(256)S(1)} %bitcast.427, f32[4,9]{1,0:T(4,128)S(1)} %slice.1030, f32[256]{0:T(256)S(1)} %bitcast.421, f32[4,68]{1,0:T(4,128)S(1)} %slice.1029), kind=kLoop, calls=%fused_computation.368 | loop fusion | flops 4386816 | bytes 2512096 | tf_op jit(solution)/shard_map/cos | solution.py:172
  171.3 4.6 cos.11
  177.6 2.6 broadcast_in_dim.14
  180.2 96.2 %while.27 = (s32[]{:T(128)}, f32[4,32,256]{2,1,0:T(8,128)S(1)}, f32[4,68,9,256]{3,2,1,0:T(8,128)}, s32[]{:T(128)}, s32[]{:T(128)}, /*index=5*/bf16[12,104,256]{2...) while((s32[]{:T(128)}, f32[4,32,256]{2,1,0:T(8,128)S(1)}, ...), condition=%wide.region_41.42_spmd, body=%wide.region_4.41_spmd.sunk | while | flops 7221273 | bytes 6562401 | solution.py:121
  197.4 1.8 fusion.274
  276.5 3.2 reshape.1111
  279.7 3.3 multiply_reduce_fusion
  283.0 4.0 fusion.236
  287.0 11.6 %fusion.254 = (f32[256]{0:T(256)S(1)}, f32[2448,256]{1,0:T(8,128)S(1)}) fusion(f32[7344,256]{1,0:T(8,128)} %get-tuple-element.372, bf16[256,256]{1,0:T(8,128)(2,1)S(1)} %copy-done.5, f32[2448,256]{1,0:T(8,128)S(1)} %reshape.1111, f32[2448]{0:T(1024)S(1)} %copy-done.7), kind=kOutput, calls=%fused_computation.432 | convolution fusion | flops 1927065344 | bytes 7662144 | tf_op jit(solution)/shard_map/dot_general | solution.py:155
  301.2 3.8 fusion.233
  305.9 43.7 %while.26 = (s32[]{:T(128)}, f32[4,32,256]{2,1,0:T(8,128)S(1)}, s32[]{:T(128)}, s32[]{:T(128)}, bf16[12,104,256]{2,1,0:T(8,128)(2,1)S(1)}, /*index=5*/bf16[12,68...) while((s32[]{:T(128)}, f32[4,32,256]{2,1,0:T(8,128)S(1)}, ...), condition=%wide.region_2.3_spmd, body=%wide.region_1.2_spmd.sunk | while | flops 3575834 | bytes 2990641 | solution.py:145
  350.9 1.9 convolution_multiply_fusion.2
  352.8 81.3 %all-reduce.1 = (f32[3,256]{1,0:T(4,128)}, f32[256]{0:T(256)}, f32[256]{0:T(256)}, f32[256]{0:T(256)}) all-reduce(f32[3,256]{1,0:T(4,128)S(1)} %convolution_multiply_fusion.2, f32[256]{0:T(256)} %broadcast_multiply_fusion.2, f32[256]{0:T(256)} %broadcast_multiply_fusion.1, ...), channel_id=1, replica_groups=mesh['lon'=32,'lat'=8] {'lon','lat'}, use_global_device_ids=true, to_apply=%region_43.44 | all-reduce | flops 1536 | bytes 12288 | tf_op jit(solution)/shard_map/psum | solution.py:246
  434.2 176.7 %all-reduce.5.cloned.1.call-done = (f32[256,256]{1,0:T(8,128)}, f32[256,256]{1,0:T(8,128)}, f32[256,256]{1,0:T(8,128)}) async-done(((f32[256,256]{1,0:T(8,128)}, f32[256,256]{1,0:T(8,128)}, f32[256,256]{1,0:T(8,128)}), (f32[256,256]{1,0:T(8,128)}, f32[256,256]{1,0:T(8,128)}, f32[256,256]{1,0:T(8,128)})) %all-reduce.5.cloned.1.call-update) | async-done | bytes 786448 | tf_op jit(solution)/shard_map/psum | solution.py:246
  (866 shorter events, 160.8 us)
Async XLA Ops:
  7.2 46.2 %copy-start = (bf16[256,256]{1,0:T(8,128)(2,1)S(1)}, bf16[256,256]{1,0:T(8,128)(2,1)}, u32[]{:S(2)}) copy-start(bf16[256,256]{1,0:T(8,128)(2,1)} %param.20) | copy-start | bytes 393220
  7.2 46.2 %copy-start.9 = (f32[256]{0:T(256)S(1)}, f32[256]{0:T(256)}, u32[]{:S(2)}) copy-start(f32[256]{0:T(256)} %param.19) | copy-start | bytes 3076
  7.2 46.2 %copy-start.11 = (f32[256]{0:T(256)S(1)}, f32[256]{0:T(256)}, u32[]{:S(2)}) copy-start(f32[256]{0:T(256)} %param.21) | copy-start | bytes 3076
  7.2 603.7 %all-reduce.5.cloned.1.call-start = ((), (), s32[]{:S(2)}) async-start(), calls=%async_computation | async-start | bytes 1572864 | tf_op jit(solution)/shard_map/psum | solution.py:246
  9.3 113.6 %collective-permute-start = (bf16[4,32,2,256]{3,1,0,2:T(8,128)(2,1)S(1)}, bf16[4,32,2,256]{3,1,0,2:T(8,128)(2,1)S(1)}, u32[]{:S(2)}, u32[]{:S(2)}) collective-permute-start(bf16[4,32,2,256]{3,1,0,2:T(8,128)(2,1)S(1)} %pad_maximum_fusion.1), channel_id=1, source_target_pairs={{0,1},{1,2},{2,3},{3,4},{4,5},{5,6},{6,7},{8,9},{9,10},{10,11},{11... | collective-permute-start | bytes 393224 | tf_op jit(solution)/shard_map/ppermute | solution.py:22
  13.2 109.7 %collective-permute-start.1 = (bf16[4,32,2,256]{3,1,0,2:T(8,128)(2,1)S(1)}, bf16[4,32,2,256]{3,1,0,2:T(8,128)(2,1)S(1)}, u32[]{:S(2)}, u32[]{:S(2)}) collective-permute-start(bf16[4,32,2,256]{3,1,0,2:T(8,128)(2,1)S(1)} %pad_maximum_fusion.1), channel_id=1, source_target_pairs={{1,0},{2,1},{3,2},{4,3},{5,4},{6,5},{7,6},{9,8},{10,9},{11,10},{12... | collective-permute-start | bytes 393224 | tf_op jit(solution)/shard_map/ppermute | solution.py:25
  53.4 54.5 %copy-start.4 = (bf16[256,256]{1,0:T(8,128)(2,1)S(1)}, bf16[256,256]{1,0:T(8,128)(2,1)}, u32[]{:S(2)}) copy-start(bf16[256,256]{1,0:T(8,128)(2,1)} %param.22) | copy-start | bytes 393220
  53.4 54.5 %copy-start.10 = (f32[256]{0:T(256)S(1)}, f32[256]{0:T(256)}, u32[]{:S(2)}) copy-start(f32[256]{0:T(256)} %param.23) | copy-start | bytes 3076
  106.1 1.8 copy-start.2
  112.1 10.8 %copy-start.3 = (bf16[4,32,256]{2,1,0:T(8,128)(2,1)S(1)}, bf16[4,32,256]{2,1,0:T(8,128)(2,1)}, u32[]{:S(2)}) copy-start(bf16[4,32,256]{2,1,0:T(8,128)(2,1)} %param.15) | copy-start | bytes 196612
  123.7 11.6 %copy-start.8 = (s32[32]{0:T(128)S(1)}, s32[32]{0:T(128)}, u32[]{:S(2)}) copy-start(s32[32]{0:T(128)} %param.24) | copy-start | bytes 388
  123.7 52.2 %collective-permute-start.2 = (bf16[12,32,2,256]{3,1,0,2:T(8,128)(2,1)}, bf16[12,32,2,256]{3,1,0,2:T(8,128)(2,1)}, u32[]{:S(2)}, u32[]{:S(2)}) collective-permute-start(bf16[12,32,2,256]{3,1,0,2:T(8,128)(2,1)} %pad_maximum_fusion), channel_id=1, source_target_pairs={{0,8},{8,16},{16,24},{24,32},{32,40},{40,48},{48,56},{56,64},{64,7... | collective-permute-start | bytes 1179656 | tf_op jit(solution)/shard_map/ppermute | solution.py:22
  127.0 48.9 %collective-permute-start.3 = (bf16[12,32,2,256]{3,1,0,2:T(8,128)(2,1)}, bf16[12,32,2,256]{3,1,0,2:T(8,128)(2,1)}, u32[]{:S(2)}, u32[]{:S(2)}) collective-permute-start(bf16[12,32,2,256]{3,1,0,2:T(8,128)(2,1)} %pad_maximum_fusion), channel_id=1, source_target_pairs={{8,0},{16,8},{24,16},{32,24},{40,32},{48,40},{56,48},{64,56},{72,6... | collective-permute-start | bytes 1179656 | tf_op jit(solution)/shard_map/ppermute | solution.py:25
  140.7 10.1 %slice-start = ((bf16[12,68,9,256]{3,2,1,0:T(8,128)(2,1)}), bf16[4,68,9,256]{3,2,1,0:T(8,128)(2,1)S(1)}, s32[]{:S(2)}) async-start(bf16[12,68,9,256]{3,2,1,0:T(8,128)(2,1)} %multiply_convert_fusion), calls=%async_computation.1 | async-start | bytes 4456448 | tf_op jit(solution)/shard_map/slice | solution.py:219
  279.6 3.3 copy-start.7
  279.6 7.3 %copy-start.5 = (bf16[256,256]{1,0:T(8,128)(2,1)S(1)}, bf16[256,256]{1,0:T(8,128)(2,1)}, u32[]{:S(2)}) copy-start(bf16[256,256]{1,0:T(8,128)(2,1)} %param.22) | copy-start | bytes 393220
  287.0 11.6 %copy-start.1 = (f32[2448,256]{1,0:T(8,128)S(1)}, f32[2448,256]{1,0:T(8,128)}, u32[]{:S(2)}) copy-start(f32[2448,256]{1,0:T(8,128)} %cos.11) | copy-start | bytes 7520260
  300.0 4.9 copy-start.6
Sparse Core Ops, SparseCore 0:
  349.7 261.1 all-reduce.4
where the time goes:
time: 626 us; the launch traced here: 623 us
  other arithmetic  192 us (31%)
  waiting for transfers between devices  177 us (28%)
  matrix products  81.7 us (13%)
  blocking collectives  81.3 us (13%)
  local copies, waits for them, and re-layouts  58.8 us (9%)
  between operations  17.1 us (3%)
  starting transfers between devices  8.56 us (1%)
  loops' own time  6.34 us (1%)
    psum x1, waiting for transfers between devices, shards(): lax.psum((grad_mix * inverse, gradients[0] * inverse, gradients[1] * inve...  177 us
    psum x1, blocking collectives, shards(): lax.psum((grad_mix * inverse, gradients[0] * inverse, gradients[1] * inve...  81.3 us
    dot_general x1, matrix products, tap_kernels(): jnp.dot(hidden_first, hidden_weight, preferred_element_type=jnp.float32)  52.7 us
    reduce_sum x17, other arithmetic, forward_one_group(): per_row.append(jnp.sum(source * mixed_cot.astype(jnp.float32), axis=1))  30.6 us
    convert_element_type x1, other arithmetic, tap_kernels(): hidden_first = jnp.sin(first_omega * pre_first).astype(jnp.bfloat16)  29.9 us
    add x17, other arithmetic, forward_one_group(): total = total + source * kern_block[:, t, a][:, None, :].astype(jnp.float32)  24.9 us
    add x17, other arithmetic, backward_one_group(): total + shifted[row_from:row_from + lat_rows].astype(jnp.float32) * kern_...  24.7 us
    convert_element_type x17, other arithmetic, backward_one_group(): kern_block[row_from:row_from + lat_rows, t, a][:, None, :]  18 us
  transfers between devices with their start and end apart: 5, of which 1 were waited for; matrix products, arithmetic and copies ran while one was open for 25% of the time, Pallas kernels for 0%

commit v1 on v0

v1 whole, which is shorter than its diff:
```python
import math

import jax
import jax.numpy as jnp
import numpy as np
from jax import lax
from jax.experimental import pallas as pl
from jax.experimental.pallas import tpu as pltpu
from jax.sharding import PartitionSpec as P

HLON = 32
HLAT = 4
NLAT = 32
NLON = 1024
ROWS = 4
COLS = 32
EXT = ROWS + 2 * HLAT
C = 256
HALF = 128
TAPS = 72
TLAT = 2 * HLAT + 1
GROUP = 4
SPAN = GROUP * TAPS
SLOTS = 56
OWN = ROWS * TLAT
WIN = 76
LINE = 104
PACK = 3 * C + HALF
MAGIC = 12582912.0
TURN = 1.0 / (2.0 * math.pi)

f32 = jnp.float32
bf16 = jnp.bfloat16

SIN_POLY = (0.99999995, -19.73917132, 64.93458165, -85.24010036, 56.24054044)
COS_POLY = (6.28318528, -41.34168067, 81.60248074, -76.58128456, 39.76072208)


def tables():
    out = np.zeros((4, 64), np.float32)
    width = np.arange(1, 64)
    out[0, 1:] = 1.0 / width
    out[1, :] = 1.0 / np.sqrt(2.0 * np.arange(64) + 1.0)
    out[2, :NLAT] = np.sin(np.pi * ((np.arange(NLAT) + 0.5) / NLAT - 0.5))
    return out


def horner(u, poly):
    total = poly[-1] * u + poly[-2]
    for c in poly[-3::-1]:
        total = total * u + c
    return total


def sine_cosine(turns):
    part = turns - ((turns + MAGIC) - MAGIC)
    h = jnp.abs(part) - 0.25
    u = h * h
    s = horner(u, SIN_POLY)
    return jnp.where(part < 0, -s, s), -h * horner(u, COS_POLY)


def reduce_eight(parts, masks):
    for shift, mask in zip((1, 2, 4), masks):
        merged = []
        for i in range(0, len(parts), 2):
            x, y = parts[i], parts[i + 1]
            merged.append(jnp.where(mask, x, y) + pltpu.roll(jnp.where(mask, y, x), 8 - shift, 0))
        parts = merged
    return parts[0]


def body(
    base_ref, lon_ref, lat_ref, tab_ref,
    field_ref, cot_ref, mix_ref, fw_ref, vec_ref, hw_ref, ow_ref,
    gfield_ref, pack_ref,
    slot_row, slot_tap, first_slot, low_tap, high_tap,
    line, fwin, mwin, kern, grad, sin_lon, cos_lon, sin_lat, cos_lat,
    h1_ref, h2_ref, c2_ref, conv, back, d_out, d_hid, d_small,
):
    base = base_ref[0]
    inverse = 1.0 / math.sqrt(NLAT * NLON)

    def grid_row(e):
        return base + e - HLAT

    def in_grid(e):
        i = grid_row(e)
        return jnp.logical_and(i >= 0, i < NLAT)

    def safe_row(e):
        return jnp.clip(grid_row(e), 0, NLAT - 1)

    def add_slots(e, lo, hi, count):
        low_tap[e] = lo
        high_tap[e] = hi
        first_slot[e] = count - lo

        def add(a, n):
            slot_row[n] = e
            slot_tap[n] = a
            return n + 1

        return lax.fori_loop(lo, hi + 1, add, count)

    def own_slots(r, count):
        e = r + HLAT
        i = grid_row(e)
        h = lat_ref[i]
        return add_slots(e, jnp.maximum(-h, -i), jnp.minimum(h, NLAT - 1 - i), count)

    own_count = lax.fori_loop(0, ROWS, own_slots, 0)

    def edge_slots(t, count):
        e = jnp.where(t < HLAT, t, t + ROWS)
        h = lat_ref[safe_row(e)]
        lo = jnp.maximum(-h, HLAT - e)
        hi = jnp.minimum(h, HLAT + ROWS - 1 - e)
        hi = jnp.where(in_grid(e), hi, lo - 1)
        return add_slots(e, lo, hi, count)

    slot_count = lax.fori_loop(0, 2 * HLAT, edge_slots, own_count)

    tap_index = lax.broadcasted_iota(jnp.int32, (TAPS, C), 0)
    lat_index = (lax.broadcasted_iota(jnp.int32, (16, C), 0) - HLAT).astype(f32)
    fw = fw_ref[...]
    vec = vec_ref[...]
    omega = 30.0 * TURN

    def angles(e, _):
        @pl.when(in_grid(e))
        def _():
            i = safe_row(e)
            w = lon_ref[i]
            lon = (tap_index - w).astype(f32) * tab_ref[0, w]
            phase = (lon * fw[0:1] + (tab_ref[2, i] * fw[2:3] + vec[0:1])) * omega
            s, c = sine_cosine(phase)
            sin_lon[e] = s
            cos_lon[e] = c
            s, c = sine_cosine((lat_index * tab_ref[0, lat_ref[i]]) * fw[1:2] * omega)
            sin_lat[e] = s
            cos_lat[e] = c

        return 0

    lax.fori_loop(0, EXT, angles, 0)

    def windows(source, target, front):
        def one(e, _):
            @pl.when(in_grid(e))
            def _():
                for h in range(2):
                    line[h, 0:8] = jnp.zeros((8, HALF), f32)
                    line[h, 96:LINE] = jnp.zeros((LINE - 96, HALF), f32)
                    line[h, front:front + 96] = source[e, :, h * HALF:(h + 1) * HALF].astype(f32)
                for h in range(2):
                    for p in range(WIN):
                        target[e, h, p] = line[h, pl.ds(p, 8, stride=4), :]

            return 0

        lax.fori_loop(0, EXT, one, 0)

    windows(field_ref, fwin, 0)
    windows(cot_ref, mwin, 8)

    def network(g, _):
        pos = [jnp.minimum(GROUP * g + q, slot_count - 1) for q in range(GROUP)]
        rows = [slot_row[n] for n in pos]
        hidden = []
        for n, e in zip(pos, rows):
            t = slot_tap[n] + HLAT
            hidden.append(sin_lon[e] * cos_lat[e, pl.ds(t, 1), :] + cos_lon[e] * sin_lat[e, pl.ds(t, 1), :])
        h1 = jnp.concatenate(hidden, axis=0).astype(bf16)
        pre = (jnp.dot(h1, hw_ref[...], preferred_element_type=f32) + vec[1:2]) * TURN
        s, c = sine_cosine(pre)
        h2 = s.astype(bf16)
        h1_ref[g] = h1
        h2_ref[g] = h2
        c2_ref[g] = c
        raw = jnp.dot(h2, ow_ref[...], preferred_element_type=f32) + vec[2:3]
        for q in range(GROUP):
            i = safe_row(rows[q])
            w = lon_ref[i]
            norm = tab_ref[1, w] * tab_ref[1, lat_ref[i]]
            k = jnp.where(tap_index <= 2 * w, raw[q * TAPS:(q + 1) * TAPS] * norm, 0.0)
            k = k.astype(bf16).astype(f32)
            at = pl.multiple_of((GROUP * g + q) * TAPS, 8)
            kern[0, pl.ds(at, TAPS), :] = k[:, :HALF]
            kern[1, pl.ds(at, TAPS), :] = k[:, HALF:]
        return 0

    lax.fori_loop(0, (slot_count + GROUP - 1) // GROUP, network, 0)

    sub = lax.broadcasted_iota(jnp.int32, (8, HALF), 0)
    masks = [(sub & bit) == 0 for bit in (1, 2, 4)]

    def conv_row(r, _):
        e = r + HLAT
        w = lon_ref[grid_row(e)]
        blocks = (2 * w + 8) // 8
        mine = [[mwin[e, h, HLON + 8 + t] for t in range(4)] for h in range(2)]

        def one_lat(a, total):
            slot = first_slot[e] + a

            def one_block(b, total):
                new = []
                start = HLON - w + 8 * b
                at = slot * TAPS + 8 * b
                for h in range(2):
                    acc = list(total[4 * h:4 * h + 4])
                    parts = []
                    x = [fwin[e + a, h, start + t] for t in range(11)]
                    for k in range(8):
                        kv = kern[h, pl.ds(at + k, 8, stride=0), :]
                        for t in range(4):
                            acc[t] = acc[t] + x[k + t] * kv
                        p = [x[k + t] * mine[h][t] for t in range(4)]
                        parts.append((p[0] + p[1]) + (p[2] + p[3]))
                    grad[h, pl.ds(pl.multiple_of(at, 8), 8), :] = reduce_eight(parts, masks)
                    new += acc
                return tuple(new)

            return lax.fori_loop(0, blocks, one_block, total)

        zero = jnp.zeros((8, HALF), f32)
        total = lax.fori_loop(low_tap[e], high_tap[e] + 1, one_lat, (zero,) * 8)
        for h in range(2):
            for t in range(4):
                conv[h, pl.ds(r * COLS + t, 8, stride=4), :] = total[4 * h + t]
        return 0

    lax.fori_loop(0, ROWS, conv_row, 0)

    def back_row(r, _):
        def one_source(e, total):
            a = r + HLAT - e
            i = safe_row(e)
            w = lon_ref[i]
            live = jnp.logical_and(in_grid(e), jnp.abs(a) <= lat_ref[i])
            blocks = jnp.where(live, (2 * w + 8) // 8, 0)
            slot = first_slot[e] + a

            def one_block(b, total):
                new = []
                start = HLON + 1 + w - 8 * b
                at = slot * TAPS + 8 * b
                for h in range(2):
                    acc = list(total[4 * h:4 * h + 4])
                    x = [mwin[e, h, start + t] for t in range(11)]
                    for k in range(8):
                        kv = kern[h, pl.ds(at + k, 8, stride=0), :]
                        for t in range(4):
                            acc[t] = acc[t] + x[7 - k + t] * kv
                    new += acc
                return tuple(new)

            return lax.fori_loop(0, blocks, one_block, total)

        zero = jnp.zeros((8, HALF), f32)
        total = lax.fori_loop(r, r + TLAT, one_source, (zero,) * 8)
        for h in range(2):
            for t in range(4):
                back[h, pl.ds(r * COLS + t, 8, stride=4), :] = total[4 * h + t]
        return 0

    lax.fori_loop(0, ROWS, back_row, 0)
    for h in range(2):
        gfield_ref[:, h * HALF:(h + 1) * HALF] = back[h].astype(bf16)
        got = lax.dot_general(
            conv[h].astype(bf16), mix_ref[...], (((0,), (0,)), ((), ())), preferred_element_type=f32
        )
        pack_ref[h * HALF:(h + 1) * HALF, 0:C] = (got * inverse).astype(bf16)

    d_out[...] = jnp.zeros_like(d_out)
    d_hid[...] = jnp.zeros_like(d_hid)
    d_small[...] = jnp.zeros_like(d_small)

    def adjoint(g, _):
        raw = []
        pos = [jnp.minimum(GROUP * g + q, own_count - 1) for q in range(GROUP)]
        rows = [slot_row[n] for n in pos]
        for q in range(GROUP):
            i = grid_row(rows[q])
            w = lon_ref[i]
            norm = tab_ref[1, w] * tab_ref[1, lat_ref[i]]
            limit = jnp.where(GROUP * g + q < own_count, 2 * w, -1)
            at = pl.multiple_of(pos[q] * TAPS, 8)
            part = jnp.concatenate([grad[0, pl.ds(at, TAPS), :], grad[1, pl.ds(at, TAPS), :]], axis=1)
            raw.append(jnp.where(tap_index <= limit, part * norm, 0.0))
        raw = jnp.concatenate(raw, axis=0)
        raw_low = raw.astype(bf16)
        h1 = h1_ref[g]
        h2 = h2_ref[g]
        rows_by_rows = (((0,), (0,)), ((), ()))
        d_out[...] += lax.dot_general(h2, raw_low, rows_by_rows, preferred_element_type=f32)
        d_small[5:6, :] += jnp.sum(raw, axis=0, keepdims=True)
        gp = lax.dot_general(
            raw_low, ow_ref[...], (((1,), (1,)), ((), ())), preferred_element_type=f32
        ) * c2_ref[g]
        gp_low = gp.astype(bf16)
        d_hid[...] += lax.dot_general(h1, gp_low, rows_by_rows, preferred_element_type=f32)
        d_small[4:5, :] += jnp.sum(gp, axis=0, keepdims=True)
        gf = lax.dot_general(
            gp_low, hw_ref[...], (((1,), (1,)), ((), ())), preferred_element_type=f32
        )
        for q in range(GROUP):
            e = rows[q]
            i = grid_row(e)
            w = lon_ref[i]
            a = slot_tap[pos[q]]
            t = a + HLAT
            c1 = cos_lon[e] * cos_lat[e, pl.ds(t, 1), :] - sin_lon[e] * sin_lat[e, pl.ds(t, 1), :]
            gq = gf[q * TAPS:(q + 1) * TAPS] * c1
            lon = (tap_index - w).astype(f32) * tab_ref[0, w]
            total = jnp.sum(gq, axis=0, keepdims=True)
            d_small[0:1, :] += jnp.sum(gq * lon, axis=0, keepdims=True)
            d_small[1:2, :] += total * (a.astype(f32) * tab_ref[0, lat_ref[i]])
            d_small[2:3, :] += total * tab_ref[2, i]
            d_small[3:4, :] += total
        return 0

    lax.fori_loop(0, (own_count + GROUP - 1) // GROUP, adjoint, 0)
    pack_ref[:, C:2 * C] = (d_hid[...] * inverse).astype(bf16)
    pack_ref[:, 2 * C:3 * C] = (d_out[...] * inverse).astype(bf16)
    d_small[0:4, :] = d_small[0:4, :] * 30.0
    pack_ref[:, 3 * C:] = jnp.transpose(d_small[...] * inverse).astype(bf16)


def local_pass(base, lon_half, lat_half, field, cot_mixed, cotangent, fw, vec, hw, ow):
    smem = pl.BlockSpec(memory_space=pltpu.SMEM)
    vmem = pl.BlockSpec(memory_space=pltpu.VMEM)
    groups = SLOTS // GROUP
    return pl.pallas_call(
        body,
        out_shape=(
            jax.ShapeDtypeStruct((ROWS * COLS, C), bf16),
            jax.ShapeDtypeStruct((C, PACK), bf16),
        ),
        in_specs=[smem] * 4 + [vmem] * 7,
        out_specs=(vmem, vmem),
        scratch_shapes=[
            pltpu.SMEM((SLOTS + 8,), jnp.int32),
            pltpu.SMEM((SLOTS + 8,), jnp.int32),
            pltpu.SMEM((16,), jnp.int32),
            pltpu.SMEM((16,), jnp.int32),
            pltpu.SMEM((16,), jnp.int32),
            pltpu.VMEM((2, LINE, HALF), f32),
            pltpu.VMEM((EXT, 2, WIN, 8, HALF), f32),
            pltpu.VMEM((EXT, 2, WIN, 8, HALF), f32),
            pltpu.VMEM((2, SLOTS * TAPS, HALF), f32),
            pltpu.VMEM((2, OWN * TAPS, HALF), f32),
            pltpu.VMEM((EXT, TAPS, C), f32),
            pltpu.VMEM((EXT, TAPS, C), f32),
            pltpu.VMEM((EXT, 16, C), f32),
            pltpu.VMEM((EXT, 16, C), f32),
            pltpu.VMEM((groups, SPAN, C), bf16),
            pltpu.VMEM((groups, SPAN, C), bf16),
            pltpu.VMEM((groups, SPAN, C), f32),
            pltpu.VMEM((2, ROWS * COLS, HALF), f32),
            pltpu.VMEM((2, ROWS * COLS, HALF), f32),
            pltpu.VMEM((C, C), f32),
            pltpu.VMEM((C, C), f32),
            pltpu.VMEM((HALF, C), f32),
        ],
        compiler_params=pltpu.CompilerParams(vmem_limit_bytes=56 * 1024 * 1024),
        name="local_pass",
    )(base, lon_half, lat_half, jnp.asarray(tables()), field, cot_mixed, cotangent, fw, vec, hw, ow)


def extended(block, axis, dim, width, periodic):
    count = lax.axis_size(axis)
    forward = [(i, i + 1) for i in range(count - 1)]
    if periodic:
        forward.append((count - 1, 0))
    backward = [(target, source) for source, target in forward]
    low = lax.ppermute(lax.slice_in_dim(block, block.shape[dim] - width, None, axis=dim), axis, forward)
    high = lax.ppermute(lax.slice_in_dim(block, 0, width, axis=dim), axis, backward)
    return jnp.concatenate([low, block, high], axis=dim)


def spread(block, axis):
    return lax.all_to_all(block, axis, 0, 0, tiled=True)


def total_of(pack):
    rows, width = pack.shape
    lat, lon = lax.axis_size("lat"), lax.axis_size("lon")
    part = spread(pack.reshape(lat, rows // lat, width), "lat")
    part = jnp.sum(part.astype(f32), axis=0).astype(bf16)
    line = spread(part, "lon")
    line = jnp.sum(line.astype(f32), axis=0, keepdims=True).astype(bf16)
    part = spread(jnp.broadcast_to(line, (lon, width)), "lon")
    full = spread(jnp.broadcast_to(part[None], (lat, lon, width)), "lat")
    return full.reshape(rows, width)


def shards(
    field, cotangent, mix_weight, first_weight, first_bias, hidden_weight, hidden_bias,
    output_weight, output_bias, lon_half, lat_half,
):
    flat_cot = cotangent.reshape(-1, C)
    mixed = lax.dot_general(
        flat_cot, mix_weight, (((1,), (1,)), ((), ())), preferred_element_type=f32
    ).astype(bf16).reshape(ROWS, COLS, C)
    both = jnp.stack((field, mixed), axis=0)
    both = extended(both, "lat", 1, HLAT, False)
    both = extended(both, "lon", 2, HLON, True)
    base = (lax.axis_index("lat") * ROWS).astype(jnp.int32).reshape(1)
    vec = jnp.stack((first_bias, hidden_bias, output_bias), axis=0)
    grad_field, pack = local_pass(
        base, lon_half, lat_half, both[0], both[1], flat_cot, first_weight, vec,
        hidden_weight, output_weight,
    )
    summed = total_of(pack).astype(f32)
    small = summed[:, 3 * C:3 * C + 8].T
    return (
        grad_field.reshape(ROWS, COLS, C),
        summed[:, :C],
        small[0:3],
        small[3],
        summed[:, C:2 * C],
        small[4],
        summed[:, 2 * C:3 * C],
        small[5],
    )


def solution(mesh):
    in_specs = (P("lat", "lon", None), P("lat", "lon", None)) + (P(),) * 9
    out_specs = (P("lat", "lon", None),) + (P(),) * 7
    return jax.shard_map(shards, mesh=mesh, in_specs=in_specs, out_specs=out_specs, check_vma=False)
```

time: 626 us -> 116 us (0.19)
  other arithmetic: 192 us -> 4.32 us
  waiting for transfers between devices: 177 us -> 18.4 us
  matrix products: 81.7 us -> 1.03 us
  local copies, waits for them, and re-layouts: 58.8 us -> 5.59 us
  blocking collectives: 81.3 us -> 53.9 us
  Pallas kernels: 0 us -> 21.7 us
  between operations: 17.1 us -> 0.78 us
  loops' own time: 6.34 us -> 0 us
    psum x1 -> x0, waiting for transfers between devices: 177 us -> none  [shards(): lax.psum((grad_mix * inverse, gradients[0] * inverse, gradients[1] * inve...]
    psum x1 -> x0, blocking collectives: 81.3 us -> none  [shards(): lax.psum((grad_mix * inverse, gradients[0] * inverse, gradients[1] * inve...]
    dot_general x8 -> x0, matrix products: 80.6 us -> none  [the longest x1 52.7 us: tap_kernels(): jnp.dot(hidden_first, hidden_weight, preferred_element_type=jnp.float32)]
    convert_element_type x41 -> x1, other arithmetic: 72.1 us -> 0.1 us  [shards(): summed = total_of(pack).astype(f32)]
    all_to_all x0 -> x4, blocking collectives: none -> 53.9 us  [spread(): return lax.all_to_all(block, axis, 0, 0, tiled=True)]
    add x34 -> x0, other arithmetic: 49.6 us -> none  [the longest x17 24.9 us: forward_one_group(): total = total + source * kern_block[:, t, a][:, None, :].astype(jnp.float32)]
    reduce_sum x18 -> x2, other arithmetic: 33.9 us -> 0.18 us  [the longest x1 0.12 us: total_of(): line = jnp.sum(line.astype(f32), axis=0, keepdims=True).astype(bf16)]
    pallas_call x0 -> x1, Pallas kernels: none -> 21.7 us  [local_pass(): pl.pallas_call(body, out_shape=(jax.ShapeDtypeStruct((ROWS * COLS, C), bf...]
  transfers between devices with their start and end apart: 5 -> 4, of which waited for: 1 -> 4; matrix products, arithmetic and copies ran while one was open for 25% -> 1% of each run, Pallas kernels for 0% -> 0%
where the time goes in v1:
time: 116 us; the launch traced here: 115 us
  blocking collectives  53.9 us (46%)
  Pallas kernels  21.7 us (19%)
  waiting for transfers between devices  18.4 us (16%)
  starting transfers between devices  9.07 us (8%)
  local copies, waits for them, and re-layouts  5.59 us (5%)
  other arithmetic  4.32 us (4%)
    all_to_all x4, blocking collectives, spread(): return lax.all_to_all(block, axis, 0, 0, tiled=True)  53.9 us
    pallas_call x1, Pallas kernels, local_pass(): pl.pallas_call(body, out_shape=(jax.ShapeDtypeStruct((ROWS * COLS, C), bf...  21.7 us
    ppermute x2, waiting for transfers between devices, extended(): lax.ppermute(lax.slice_in_dim(block, 0, width, axis=dim), axis, backward)  9.21 us
    ppermute x2, waiting for transfers between devices, extended(): lax.ppermute(lax.slice_in_dim(block, block.shape[dim] - width, None, axis...  9.16 us
    ppermute x2, starting transfers between devices, extended(): lax.ppermute(lax.slice_in_dim(block, block.shape[dim] - width, None, axis...  7.78 us
  transfers between devices with their start and end apart: 4, of which 4 were waited for; matrix products, arithmetic and copies ran while one was open for 1% of the time, Pallas kernels for 0%

profile of v1, /device:TPU:1, one launch (start us, length us, event | category | flops | bytes accessed | tf_op | source)
XLA Modules:
  0.0 114.8 jit_solution(18439132277975655427)
XLA Ops:
  0.7 0.9 copy-done
  1.6 1.0 convolution_convert_fusion
  2.6 0.9 pad_maximum_fusion.2
  3.5 3.9 %collective-permute-start = (bf16[2,4,32,256]{3,2,1,0:T(8,128)(2,1)S(1)}, bf16[2,4,32,256]{3,2,1,0:T(8,128)(2,1)S(1)}, u32[]{:S(2)}, u32[]{:S(2)}) collective-permute-start(bf16[2,4,32,256]{3,2,1,0:T(8,128)(2,1)S(1)} %pad_maximum_fusion.2), channel_id=1, source_target_pairs={{0,1},{1,2},{2,3},{3,4},{4,5},{5,6},{6,7},{8,9},{9,10},{10,11},{11... | collective-permute-start | bytes 393224 | tf_op jit(solution)/shard_map/ppermute | solution.py:378
  7.4 1.3 %collective-permute-start.1 = (bf16[2,4,32,256]{3,2,1,0:T(8,128)(2,1)S(1)}, bf16[2,4,32,256]{3,2,1,0:T(8,128)(2,1)S(1)}, u32[]{:S(2)}, u32[]{:S(2)}) collective-permute-start(bf16[2,4,32,256]{3,2,1,0:T(8,128)(2,1)S(1)} %pad_maximum_fusion.2), channel_id=1, source_target_pairs={{1,0},{2,1},{3,2},{4,3},{5,4},{6,5},{7,6},{9,8},{10,9},{11,10},{12... | collective-permute-start | bytes 393224 | tf_op jit(solution)/shard_map/ppermute | solution.py:379
  8.7 0.9 collective-permute-done
  9.6 5.2 %collective-permute-done.1 = bf16[2,4,32,256]{3,2,1,0:T(8,128)(2,1)S(1)} collective-permute-done((bf16[2,4,32,256]{3,2,1,0:T(8,128)(2,1)S(1)}, bf16[2,4,32,256]{3,2,1,0:T(8,128)(2,1)S(1)}, u32[]{:S(2)}, u32[]{:S(2)}) %collective-permute-start.1) | collective-permute-done | bytes 131104 | tf_op jit(solution)/shard_map/ppermute | solution.py:379
  14.8 0.9 pad_maximum_fusion.1
  15.7 3.8 %collective-permute-start.2 = (bf16[2,12,32,256]{3,2,1,0:T(8,128)(2,1)S(1)}, bf16[2,12,32,256]{3,2,1,0:T(8,128)(2,1)S(1)}, u32[]{:S(2)}, u32[]{:S(2)}) collective-permute-start(bf16[2,12,32,256]{3,2,1,0:T(8,128)(2,1)S(1)} %pad_maximum_fusion.1), channel_id=1, source_target_pairs={{0,8},{8,16},{16,24},{24,32},{32,40},{40,48},{48,56},{56,64},{64,7... | collective-permute-start | bytes 1179656 | tf_op jit(solution)/shard_map/ppermute | solution.py:378
  19.5 0.6 pad_maximum_fusion.3.vec_ref
  20.1 8.3 %collective-permute-done.2 = bf16[2,12,32,256]{3,2,1,0:T(8,128)(2,1)S(1)} collective-permute-done((bf16[2,12,32,256]{3,2,1,0:T(8,128)(2,1)S(1)}, bf16[2,12,32,256]{3,2,1,0:T(8,128)(2,1)S(1)}, u32[]{:S(2)}, u32[]{:S(2)}) %collective-permute-start.2) | collective-permute-done | bytes 393248 | tf_op jit(solution)/shard_map/ppermute | solution.py:378
  28.4 4.0 %collective-permute-done.3 = bf16[2,12,32,256]{3,2,1,0:T(8,128)(2,1)S(1)} collective-permute-done((bf16[2,12,32,256]{3,2,1,0:T(8,128)(2,1)S(1)}, bf16[2,12,32,256]{3,2,1,0:T(8,128)(2,1)S(1)}, u32[]{:S(2)}, u32[]{:S(2)}) %collective-permute-start.3) | collective-permute-done | bytes 393248 | tf_op jit(solution)/shard_map/ppermute | solution.py:379
  32.5 1.1 slice_bitcast_fusion
  33.6 21.7 %local_pass.1 = (bf16[128,256]{1,0:T(8,128)(2,1)}, bf16[256,896]{1,0:T(8,128)(2,1)}) custom-call(s32[1]{0:T(128)} %bitcast.base_ref, s32[32]{0:T(128)} %lon_ref.1, s32[32]{0:T(128)} %lat_ref.1, f32[4,64]{1,0:T(4,128)} %constant.12.clone.tab_ref, bf16[12,96,256]{2,1,0:T(8,128)(2,1)} %get-tuple-element.48.field_ref, ...), custom_call_target="tpu_custom_call" | custom-call | tf_op jit(solution)/shard_map/local_pass/pallas_call | solution.py:335
  55.3 10.7 %all_to_all.25 = bf16[8,32,896]{2,1,0:T(8,128)(2,1)S(1)} all-to-all(bf16[8,32,896]{2,1,0:T(8,128)(2,1)} %bitcast.32), channel_id=1, replica_groups=mesh['lon'=32,'lat'=8] {'lat'}, dimensions={0} | all-to-all | bytes 917504 | tf_op jit(solution)/shard_map/all_to_all | solution.py:384
  66.1 0.5 broadcast.7
  66.6 0.7 reduce.9
  67.4 19.1 %all_to_all.26 = bf16[32,2,448]{2,1,0:T(2,128)(2,1)S(1)} all-to-all(bf16[32,2,448]{2,1,0:T(2,128)(2,1)S(1)} %reshape.53), channel_id=1, replica_groups=mesh['lon'=32,'lat'=8] {'lon'}, dimensions={0} | all-to-all | bytes 114688 | tf_op jit(solution)/shard_map/all_to_all | solution.py:384
  86.8 1.0 reduce.10
  87.9 12.9 %all_to_all.27 = bf16[32,2,448]{2,1,0:T(2,128)(2,1)S(1)} all-to-all(bf16[32,2,448]{2,1,0:T(2,128)(2,1)S(1)} %reshape.55), channel_id=1, replica_groups=mesh['lon'=32,'lat'=8] {'lon'}, dimensions={0} | all-to-all | bytes 114688 | tf_op jit(solution)/shard_map/all_to_all | solution.py:384
  101.0 11.2 %all_to_all.28 = bf16[8,32,896]{2,1,0:T(8,128)(2,1)S(1)} all-to-all(bf16[8,32,896]{2,1,0:T(8,128)(2,1)S(1)} %broadcast_in_dim.16), channel_id=1, replica_groups=mesh['lon'=32,'lat'=8] {'lat'}, dimensions={0} | all-to-all | bytes 917504 | tf_op jit(solution)/shard_map/all_to_all | solution.py:384
  112.3 0.9 fusion
  113.2 0.9 slice_reduce_fusion
  114.1 0.7 copy.24
  (22 shorter events, 1.0 us)
Async XLA Ops:
  0.6 0.9 copy-start
  0.6 31.8 %copy-start.1 = (bf16[4,32,256]{2,1,0:T(8,128)(2,1)S(1)}, bf16[4,32,256]{2,1,0:T(8,128)(2,1)}, u32[]{:S(2)}) copy-start(bf16[4,32,256]{2,1,0:T(8,128)(2,1)} %param.12) | copy-start | bytes 196612
  0.7 18.8 %copy-start.4 = (f32[256]{0:T(256)S(1)}, f32[256]{0:T(256)}, u32[]{:S(2)}) copy-start(f32[256]{0:T(256)} %param.16) | copy-start | bytes 3076
  0.7 18.8 %copy-start.3 = (f32[256]{0:T(256)S(1)}, f32[256]{0:T(256)}, u32[]{:S(2)}) copy-start(f32[256]{0:T(256)} %param.18) | copy-start | bytes 3076
  0.7 18.8 %copy-start.2 = (f32[256]{0:T(256)S(1)}, f32[256]{0:T(256)}, u32[]{:S(2)}) copy-start(f32[256]{0:T(256)} %param.20) | copy-start | bytes 3076
  3.5 6.1 %collective-permute-start = (bf16[2,4,32,256]{3,2,1,0:T(8,128)(2,1)S(1)}, bf16[2,4,32,256]{3,2,1,0:T(8,128)(2,1)S(1)}, u32[]{:S(2)}, u32[]{:S(2)}) collective-permute-start(bf16[2,4,32,256]{3,2,1,0:T(8,128)(2,1)S(1)} %pad_maximum_fusion.2), channel_id=1, source_target_pairs={{0,1},{1,2},{2,3},{3,4},{4,5},{5,6},{6,7},{8,9},{9,10},{10,11},{11... | collective-permute-start | bytes 393224 | tf_op jit(solution)/shard_map/ppermute | solution.py:378
  7.4 7.4 %collective-permute-start.1 = (bf16[2,4,32,256]{3,2,1,0:T(8,128)(2,1)S(1)}, bf16[2,4,32,256]{3,2,1,0:T(8,128)(2,1)S(1)}, u32[]{:S(2)}, u32[]{:S(2)}) collective-permute-start(bf16[2,4,32,256]{3,2,1,0:T(8,128)(2,1)S(1)} %pad_maximum_fusion.2), channel_id=1, source_target_pairs={{1,0},{2,1},{3,2},{4,3},{5,4},{6,5},{7,6},{9,8},{10,9},{11,10},{12... | collective-permute-start | bytes 393224 | tf_op jit(solution)/shard_map/ppermute | solution.py:379
  15.7 12.8 %collective-permute-start.2 = (bf16[2,12,32,256]{3,2,1,0:T(8,128)(2,1)S(1)}, bf16[2,12,32,256]{3,2,1,0:T(8,128)(2,1)S(1)}, u32[]{:S(2)}, u32[]{:S(2)}) collective-permute-start(bf16[2,12,32,256]{3,2,1,0:T(8,128)(2,1)S(1)} %pad_maximum_fusion.1), channel_id=1, source_target_pairs={{0,8},{8,16},{16,24},{24,32},{32,40},{40,48},{48,56},{56,64},{64,7... | collective-permute-start | bytes 1179656 | tf_op jit(solution)/shard_map/ppermute | solution.py:378
  19.5 12.9 %collective-permute-start.3 = (bf16[2,12,32,256]{3,2,1,0:T(8,128)(2,1)S(1)}, bf16[2,12,32,256]{3,2,1,0:T(8,128)(2,1)S(1)}, u32[]{:S(2)}, u32[]{:S(2)}) collective-permute-start(bf16[2,12,32,256]{3,2,1,0:T(8,128)(2,1)S(1)} %pad_maximum_fusion.1), channel_id=1, source_target_pairs={{8,0},{16,8},{24,16},{32,24},{40,32},{48,40},{56,48},{64,56},{72,6... | collective-permute-start | bytes 1179656 | tf_op jit(solution)/shard_map/ppermute | solution.py:379

commit v2 on v1

--- a/solution.py
+++ b/solution.py
@@ -6,6 +6,7 @@
 from jax import lax
 from jax.experimental import pallas as pl
 from jax.experimental.pallas import tpu as pltpu
+from jax.sharding import Mesh
 from jax.sharding import PartitionSpec as P
 
 HLON = 32
@@ -70,27 +71,20 @@
     return parts[0]
 
 
-def body(
-    base_ref, lon_ref, lat_ref, tab_ref,
-    field_ref, cot_ref, mix_ref, fw_ref, vec_ref, hw_ref, ow_ref,
-    gfield_ref, pack_ref,
-    slot_row, slot_tap, first_slot, low_tap, high_tap,
-    line, fwin, mwin, kern, grad, sin_lon, cos_lon, sin_lat, cos_lat,
-    h1_ref, h2_ref, c2_ref, conv, back, d_out, d_hid, d_small,
-):
-    base = base_ref[0]
-    inverse = 1.0 / math.sqrt(NLAT * NLON)
-
-    def grid_row(e):
-        return base + e - HLAT
-
-    def in_grid(e):
-        i = grid_row(e)
-        return jnp.logical_and(i >= 0, i < NLAT)
-
-    def safe_row(e):
-        return jnp.clip(grid_row(e), 0, NLAT - 1)
-
+def grid_row(place_ref, e):
+    return place_ref[0] + e - HLAT
+
+
+def in_grid(place_ref, e):
+    i = grid_row(place_ref, e)
+    return jnp.logical_and(i >= 0, i < NLAT)
+
+
+def safe_row(place_ref, e):
+    return jnp.clip(grid_row(place_ref, e), 0, NLAT - 1)
+
+
+def number_slots(place_ref, lat_ref, slot_row, slot_tap, first_slot, low_tap, high_tap):
     def add_slots(e, lo, hi, count):
         low_tap[e] = lo
         high_tap[e] = hi
@@ -105,7 +99,7 @@
 
     def own_slots(r, count):
         e = r + HLAT
-        i = grid_row(e)
+        i = grid_row(place_ref, e)
         h = lat_ref[i]
         return add_slots(e, jnp.maximum(-h, -i), jnp.minimum(h, NLAT - 1 - i), count)
 
@@ -113,14 +107,22 @@
 
     def edge_slots(t, count):
         e = jnp.where(t < HLAT, t, t + ROWS)
-        h = lat_ref[safe_row(e)]
+        h = lat_ref[safe_row(place_ref, e)]
         lo = jnp.maximum(-h, HLAT - e)
         hi = jnp.minimum(h, HLAT + ROWS - 1 - e)
-        hi = jnp.where(in_grid(e), hi, lo - 1)
+        hi = jnp.where(in_grid(place_ref, e), hi, lo - 1)
         return add_slots(e, lo, hi, count)
 
-    slot_count = lax.fori_loop(0, 2 * HLAT, edge_slots, own_count)
-
+    return own_count, lax.fori_loop(0, 2 * HLAT, edge_slots, own_count)
+
+
+def network_body(
+    place_ref, lon_ref, lat_ref, tab_ref, fw_ref, vec_ref, hw_ref, ow_ref,
+    kern, h1_ref, h2_ref, c2_ref, own_sin_lon, own_cos_lon, own_sin_lat, own_cos_lat,
+    slot_row, slot_tap, first_slot, low_tap, high_tap, sin_lon, cos_lon, sin_lat, cos_lat,
+):
+    own_count, slot_count = number_slots(place_ref, lat_ref, slot_row, slot_tap, first_slot, low_tap, high_tap)
+    own_groups = (own_count + GROUP - 1) // GROUP
     tap_index = lax.broadcasted_iota(jnp.int32, (TAPS, C), 0)
     lat_index = (lax.broadcasted_iota(jnp.int32, (16, C), 0) - HLAT).astype(f32)
     fw = fw_ref[...]
@@ -128,9 +130,9 @@
     omega = 30.0 * TURN
 
     def angles(e, _):
-        @pl.when(in_grid(e))
+        @pl.when(in_grid(place_ref, e))
         def _():
-            i = safe_row(e)
+            i = safe_row(place_ref, e)
             w = lon_ref[i]
             lon = (tap_index - w).astype(f32) * tab_ref[0, w]
             phase = (lon * fw[0:1] + (tab_ref[2, i] * fw[2:3] + vec[0:1])) * omega
@@ -144,25 +146,6 @@
         return 0
 
     lax.fori_loop(0, EXT, angles, 0)
-
-    def windows(source, target, front):
-        def one(e, _):
-            @pl.when(in_grid(e))
-            def _():
-                for h in range(2):
-                    line[h, 0:8] = jnp.zeros((8, HALF), f32)
-                    line[h, 96:LINE] = jnp.zeros((LINE - 96, HALF), f32)
-                    line[h, front:front + 96] = source[e, :, h * HALF:(h + 1) * HALF].astype(f32)
-                for h in range(2):
-                    for p in range(WIN):
-                        target[e, h, p] = line[h, pl.ds(p, 8, stride=4), :]
-
-            return 0
-
-        lax.fori_loop(0, EXT, one, 0)
-
-    windows(field_ref, fwin, 0)
-    windows(cot_ref, mwin, 8)
 
     def network(g, _):
         pos = [jnp.minimum(GROUP * g + q, slot_count - 1) for q in range(GROUP)]
@@ -175,12 +158,16 @@
         pre = (jnp.dot(h1, hw_ref[...], preferred_element_type=f32) + vec[1:2]) * TURN
         s, c = sine_cosine(pre)
         h2 = s.astype(bf16)
-        h1_ref[g] = h1
-        h2_ref[g] = h2
-        c2_ref[g] = c
+
+        @pl.when(g < own_groups)
+        def _():
+            h1_ref[g] = h1
+            h2_ref[g] = h2
+            c2_ref[g] = c
+
         raw = jnp.dot(h2, ow_ref[...], preferred_element_type=f32) + vec[2:3]
         for q in range(GROUP):
-            i = safe_row(rows[q])
+            i = safe_row(place_ref, rows[q])
             w = lon_ref[i]
             norm = tab_ref[1, w] * tab_ref[1, lat_ref[i]]
             k = jnp.where(tap_index <= 2 * w, raw[q * TAPS:(q + 1) * TAPS] * norm, 0.0)
@@ -191,13 +178,94 @@
         return 0
 
     lax.fori_loop(0, (slot_count + GROUP - 1) // GROUP, network, 0)
+    for own, every in (
+        (own_sin_lon, sin_lon), (own_cos_lon, cos_lon), (own_sin_lat, sin_lat), (own_cos_lat, cos_lat),
+    ):
+        own[...] = every[HLAT:HLAT + ROWS]
+
+
+def network_pass(place, lon_half, lat_half, fw, vec, hw, ow):
+    smem = pl.BlockSpec(memory_space=pltpu.SMEM)
+    vmem = pl.BlockSpec(memory_space=pltpu.VMEM)
+    return pl.pallas_call(
+        network_body,
+        out_shape=(
+            jax.ShapeDtypeStruct((2, SLOTS * TAPS, HALF), f32),
+            jax.ShapeDtypeStruct((OWN // GROUP, SPAN, C), bf16),
+            jax.ShapeDtypeStruct((OWN // GROUP, SPAN, C), bf16),
+            jax.ShapeDtypeStruct((OWN // GROUP, SPAN, C), f32),
+            jax.ShapeDtypeStruct((ROWS, TAPS, C), f32),
+            jax.ShapeDtypeStruct((ROWS, TAPS, C), f32),
+            jax.ShapeDtypeStruct((ROWS, 16, C), f32),
+            jax.ShapeDtypeStruct((ROWS, 16, C), f32),
+        ),
+        in_specs=[smem] * 4 + [vmem] * 4,
+        out_specs=(vmem,) * 8,
+        scratch_shapes=[
+            pltpu.SMEM((SLOTS + 8,), jnp.int32),
+            pltpu.SMEM((SLOTS + 8,), jnp.int32),
+            pltpu.SMEM((16,), jnp.int32),
+            pltpu.SMEM((16,), jnp.int32),
+            pltpu.SMEM((16,), jnp.int32),
+            pltpu.VMEM((EXT, TAPS, C), f32),
+            pltpu.VMEM((EXT, TAPS, C), f32),
+            pltpu.VMEM((EXT, 16, C), f32),
+            pltpu.VMEM((EXT, 16, C), f32),
+        ],
+        compiler_params=pltpu.CompilerParams(vmem_limit_bytes=22 * 1024 * 1024),
+        cost_estimate=pl.CostEstimate(flops=6_000_000_000, bytes_accessed=16_000_000, transcendentals=0),
+        name="network_pass",
+    )(place, lon_half, lat_half, jnp.asarray(tables()), fw, vec, hw, ow)
+
+
+def body(
+    place_ref, lon_ref, lat_ref, tab_ref,
+    here_ref, inner_ref, outer_ref, cot_ref, hw_ref, ow_ref,
+    kern, h1_ref, h2_ref, c2_ref, sin_lon, cos_lon, sin_lat, cos_lat,
+    gfield_ref, keep_ref, send_ref,
+    slot_row, slot_tap, first_slot, low_tap, high_tap,
+    line, fwin, mwin, grad, conv, back, d_mix, d_out, d_hid, d_small, d_side,
+):
+    inverse = 1.0 / math.sqrt(NLAT * NLON)
+    own_count, slot_count = number_slots(place_ref, lat_ref, slot_row, slot_tap, first_slot, low_tap, high_tap)
+    tap_index = lax.broadcasted_iota(jnp.int32, (TAPS, C), 0)
+    lat_odd = place_ref[2]
+    core = place_ref[1]
+    left_inner = core == 1
+
+    def windows(which, target, front):
+        def one(e, _):
+            @pl.when(in_grid(place_ref, e))
+            def _():
+                band = e // ROWS
+                part = jnp.where(band == 1, 0, jnp.where((band == 2) == (lat_odd == 1), 2, 1))
+                row = e % ROWS
+                for h in range(2):
+                    lanes = slice(h * HALF, (h + 1) * HALF)
+                    near = inner_ref[part, which, row, :, lanes].astype(f32)
+                    far = outer_ref[part, which, row, :, lanes].astype(f32)
+                    line[h, 0:8] = jnp.zeros((8, HALF), f32)
+                    line[h, 96:LINE] = jnp.zeros((LINE - 96, HALF), f32)
+                    line[h, front:front + 32] = jnp.where(left_inner, near, far)
+                    line[h, front + 32:front + 64] = here_ref[part, which, row, :, lanes].astype(f32)
+                    line[h, front + 64:front + 96] = jnp.where(left_inner, far, near)
+                for h in range(2):
+                    for p in range(WIN):
+                        target[e, h, p] = line[h, pl.ds(p, 8, stride=4), :]
+
+            return 0
+
+        lax.fori_loop(0, EXT, one, 0)
+
+    windows(0, fwin, 0)
+    windows(1, mwin, 8)
 
     sub = lax.broadcasted_iota(jnp.int32, (8, HALF), 0)
     masks = [(sub & bit) == 0 for bit in (1, 2, 4)]
 
     def conv_row(r, _):
         e = r + HLAT
-        w = lon_ref[grid_row(e)]
+        w = lon_ref[grid_row(place_ref, e)]
         blocks = (2 * w + 8) // 8
         mine = [[mwin[e, h, HLON + 8 + t] for t in range(4)] for h in range(2)]
 
@@ -236,9 +304,9 @@
     def back_row(r, _):
         def one_source(e, total):
             a = r + HLAT - e
-            i = safe_row(e)
+            i = safe_row(place_ref, e)
             w = lon_ref[i]
-            live = jnp.logical_and(in_grid(e), jnp.abs(a) <= lat_ref[i])
+            live = jnp.logical_and(in_grid(place_ref, e), jnp.abs(a) <= lat_ref[i])
             blocks = jnp.where(live, (2 * w + 8) // 8, 0)
             slot = first_slot[e] + a
 
@@ -269,9 +337,9 @@
     for h in range(2):
         gfield_ref[:, h * HALF:(h + 1) * HALF] = back[h].astype(bf16)
         got = lax.dot_general(
-            conv[h].astype(bf16), mix_ref[...], (((0,), (0,)), ((), ())), preferred_element_type=f32
+            conv[h].astype(bf16), cot_ref[...], (((0,), (0,)), ((), ())), preferred_element_type=f32
         )
-        pack_ref[h * HALF:(h + 1) * HALF, 0:C] = (got * inverse).astype(bf16)
+        d_mix[h * HALF:(h + 1) * HALF, :] = got
 
     d_out[...] = jnp.zeros_like(d_out)
     d_hid[...] = jnp.zeros_like(d_hid)
@@ -282,7 +350,7 @@
         pos = [jnp.minimum(GROUP * g + q, own_count - 1) for q in range(GROUP)]
         rows = [slot_row[n] for n in pos]
         for q in range(GROUP):
-            i = grid_row(rows[q])
+            i = grid_row(place_ref, rows[q])
             w = lon_ref[i]
             norm = tab_ref[1, w] * tab_ref[1, lat_ref[i]]
             limit = jnp.where(GROUP * g + q < own_count, 2 * w, -1)
@@ -307,11 +375,11 @@
         )
         for q in range(GROUP):
             e = rows[q]
-            i = grid_row(e)
+            i = grid_row(place_ref, e)
             w = lon_ref[i]
             a = slot_tap[pos[q]]
             t = a + HLAT
-            c1 = cos_lon[e] * cos_lat[e, pl.ds(t, 1), :] - sin_lon[e] * sin_lat[e, pl.ds(t, 1), :]
+            c1 = cos_lon[e - HLAT] * cos_lat[e - HLAT, pl.ds(t, 1), :] - sin_lon[e - HLAT] * sin_lat[e - HLAT, pl.ds(t, 1), :]
             gq = gf[q * TAPS:(q + 1) * TAPS] * c1
             lon = (tap_index - w).astype(f32) * tab_ref[0, w]
             total = jnp.sum(gq, axis=0, keepdims=True)
@@ -322,24 +390,56 @@
         return 0
 
     lax.fori_loop(0, (own_count + GROUP - 1) // GROUP, adjoint, 0)
-    pack_ref[:, C:2 * C] = (d_hid[...] * inverse).astype(bf16)
-    pack_ref[:, 2 * C:3 * C] = (d_out[...] * inverse).astype(bf16)
     d_small[0:4, :] = d_small[0:4, :] * 30.0
-    pack_ref[:, 3 * C:] = jnp.transpose(d_small[...] * inverse).astype(bf16)
-
-
-def local_pass(base, lon_half, lat_half, field, cot_mixed, cotangent, fw, vec, hw, ow):
+    d_side[...] = jnp.transpose(d_small[...])
+    for target, half in ((keep_ref, core), (send_ref, 1 - core)):
+        rows = pl.ds(pl.multiple_of(half * HALF, HALF), HALF)
+        for q, source in enumerate((d_mix, d_hid, d_out, d_side)):
+            part = source[rows, :] * inverse
+            target[:, q * C:q * C + part.shape[1]] = part.astype(bf16)
+
+
+def unpack_body(place_ref, own_ref, other_ref, mix_ref, hid_ref, out_ref, first_ref, fb_ref, hb_ref, ob_ref, side):
+    core = place_ref[1]
+    for source, half in ((own_ref, core), (other_ref, 1 - core)):
+        rows = pl.ds(pl.multiple_of(half * HALF, HALF), HALF)
+        for q, target in enumerate((mix_ref, hid_ref, out_ref)):
+            target[rows, :] = source[:, q * C:(q + 1) * C].astype(f32)
+        side[rows, :] = source[:, 3 * C:].astype(f32)
+    small = jnp.transpose(side[...])
+    first_ref[...] = small[0:3]
+    fb_ref[...] = small[3:4]
+    hb_ref[...] = small[4:5]
+    ob_ref[...] = small[5:6]
+
+
+def unpack(place, own, other):
+    vmem = pl.BlockSpec(memory_space=pltpu.VMEM)
+    square = jax.ShapeDtypeStruct((C, C), f32)
+    line = jax.ShapeDtypeStruct((1, C), f32)
+    return pl.pallas_call(
+        unpack_body,
+        out_shape=(square, square, square, jax.ShapeDtypeStruct((3, C), f32), line, line, line),
+        in_specs=[pl.BlockSpec(memory_space=pltpu.SMEM)] + [vmem] * 2,
+        out_specs=(vmem,) * 7,
+        scratch_shapes=[pltpu.VMEM((C, HALF), f32)],
+        compiler_params=pltpu.CompilerParams(vmem_limit_bytes=8 * 1024 * 1024),
+        name="unpack",
+    )(place, own, other)
+
+
+def local_pass(place, lon_half, lat_half, here, inner, outer, cotangent, hw, ow, saved):
     smem = pl.BlockSpec(memory_space=pltpu.SMEM)
     vmem = pl.BlockSpec(memory_space=pltpu.VMEM)
-    groups = SLOTS // GROUP
     return pl.pallas_call(
         body,
         out_shape=(
             jax.ShapeDtypeStruct((ROWS * COLS, C), bf16),
-            jax.ShapeDtypeStruct((C, PACK), bf16),
+            jax.ShapeDtypeStruct((C // 2, PACK), bf16),
+            jax.ShapeDtypeStruct((C // 2, PACK), bf16),
         ),
-        in_specs=[smem] * 4 + [vmem] * 7,
-        out_specs=(vmem, vmem),
+        in_specs=[smem] * 4 + [vmem] * 14,
+        out_specs=(vmem,) * 3,
         scratch_shapes=[
             pltpu.SMEM((SLOTS + 8,), jnp.int32),
             pltpu.SMEM((SLOTS + 8,), jnp.int32),
@@ -349,51 +449,48 @@
             pltpu.VMEM((2, LINE, HALF), f32),
             pltpu.VMEM((EXT, 2, WIN, 8, HALF), f32),
             pltpu.VMEM((EXT, 2, WIN, 8, HALF), f32),
-            pltpu.VMEM((2, SLOTS * TAPS, HALF), f32),
             pltpu.VMEM((2, OWN * TAPS, HALF), f32),
-            pltpu.VMEM((EXT, TAPS, C), f32),
-            pltpu.VMEM((EXT, TAPS, C), f32),
-            pltpu.VMEM((EXT, 16, C), f32),
-            pltpu.VMEM((EXT, 16, C), f32),
-            pltpu.VMEM((groups, SPAN, C), bf16),
-            pltpu.VMEM((groups, SPAN, C), bf16),
-            pltpu.VMEM((groups, SPAN, C), f32),
             pltpu.VMEM((2, ROWS * COLS, HALF), f32),
             pltpu.VMEM((2, ROWS * COLS, HALF), f32),
             pltpu.VMEM((C, C), f32),
             pltpu.VMEM((C, C), f32),
+            pltpu.VMEM((C, C), f32),
             pltpu.VMEM((HALF, C), f32),
+            pltpu.VMEM((C, HALF), f32),
         ],
-        compiler_params=pltpu.CompilerParams(vmem_limit_bytes=56 * 1024 * 1024),
+        compiler_params=pltpu.CompilerParams(vmem_limit_bytes=40 * 1024 * 1024),
+        cost_estimate=pl.CostEstimate(flops=9_000_000_000, bytes_accessed=24_000_000, transcendentals=0),
         name="local_pass",
-    )(base, lon_half, lat_half, jnp.asarray(tables()), field, cot_mixed, cotangent, fw, vec, hw, ow)
-
-
-def extended(block, axis, dim, width, periodic):
-    count = lax.axis_size(axis)
-    forward = [(i, i + 1) for i in range(count - 1)]
-    if periodic:
-        forward.append((count - 1, 0))
-    backward = [(target, source) for source, target in forward]
-    low = lax.ppermute(lax.slice_in_dim(block, block.shape[dim] - width, None, axis=dim), axis, forward)
-    high = lax.ppermute(lax.slice_in_dim(block, 0, width, axis=dim), axis, backward)
-    return jnp.concatenate([low, block, high], axis=dim)
+    )(place, lon_half, lat_half, jnp.asarray(tables()), here, inner, outer, cotangent, hw, ow, *saved)
+
+
+def swap(block, axis, pairs):
+    return lax.ppermute(block, axis, pairs)
+
+
+LAT_INNER = [(i, i ^ 1) for i in range(8)]
+LAT_OUTER = [(i, i + 1 if i % 2 else i - 1) for i in range(1, 7)]
+LON_INNER = [(i, i ^ 1) for i in range(32)]
+LON_OUTER = [(i, (i + 1 if i % 2 else i - 1) % 32) for i in range(32)]
+PLANE = ("y", "x_low", "x_high")
 
 
 def spread(block, axis):
     return lax.all_to_all(block, axis, 0, 0, tiled=True)
 
 
-def total_of(pack):
-    rows, width = pack.shape
-    lat, lon = lax.axis_size("lat"), lax.axis_size("lon")
-    part = spread(pack.reshape(lat, rows // lat, width), "lat")
-    part = jnp.sum(part.astype(f32), axis=0).astype(bf16)
-    line = spread(part, "lon")
-    line = jnp.sum(line.astype(f32), axis=0, keepdims=True).astype(bf16)
-    part = spread(jnp.broadcast_to(line, (lon, width)), "lon")
-    full = spread(jnp.broadcast_to(part[None], (lat, lon, width)), "lat")
-    return full.reshape(rows, width)
+def total_of(place, keep, send):
+    total = (keep.astype(f32) + swap(send, "core", [(0, 1), (1, 0)]).astype(f32)).astype(bf16)
+    total = spread(total.reshape(16, 8, PACK), PLANE)
+    total = jnp.sum(total.astype(f32), axis=0)
+    for bits in (1, 2, 6):
+        total = total + swap(total, "z", [(i, i ^ bits) for i in range(8)])
+    own = spread(jnp.broadcast_to(total.astype(bf16)[None], (16, 8, PACK)), PLANE).reshape(HALF, PACK)
+    return unpack(place, own, swap(own, "core", [(0, 1), (1, 0)]))
+
+
+LAT = ("y", "x_low")
+LON = ("z", "x_high", "core")
 
 
 def shards(
@@ -405,29 +502,25 @@
         flat_cot, mix_weight, (((1,), (1,)), ((), ())), preferred_element_type=f32
     ).astype(bf16).reshape(ROWS, COLS, C)
     both = jnp.stack((field, mixed), axis=0)
-    both = extended(both, "lat", 1, HLAT, False)
-    both = extended(both, "lon", 2, HLON, True)
-    base = (lax.axis_index("lat") * ROWS).astype(jnp.int32).reshape(1)
+    here = jnp.stack((both, swap(both, LAT, LAT_INNER), swap(both, LAT, LAT_OUTER)), axis=0)
+    inner = swap(here, LON, LON_INNER)
+    outer = swap(here, LON, LON_OUTER)
+    lat = lax.axis_index("y") * 2 + lax.axis_index("x_low")
+    place = jnp.stack((lat * ROWS, lax.axis_index("core"), lat % 2)).astype(jnp.int32)
     vec = jnp.stack((first_bias, hidden_bias, output_bias), axis=0)
-    grad_field, pack = local_pass(
-        base, lon_half, lat_half, both[0], both[1], flat_cot, first_weight, vec,
-        hidden_weight, output_weight,
+    saved = network_pass(place, lon_half, lat_half, first_weight, vec, hidden_weight, output_weight)
+    grad_field, keep, send = local_pass(
+        place, lon_half, lat_half, here, inner, outer, flat_cot, hidden_weight, output_weight, saved,
     )
-    summed = total_of(pack).astype(f32)
-    small = summed[:, 3 * C:3 * C + 8].T
+    mix, hid, out, first, fb, hb, ob = total_of(place, keep, send)
     return (
-        grad_field.reshape(ROWS, COLS, C),
-        summed[:, :C],
-        small[0:3],
-        small[3],
-        summed[:, C:2 * C],
-        small[4],
-        summed[:, 2 * C:3 * C],
-        small[5],
+        grad_field.reshape(ROWS, COLS, C), mix, first, fb.reshape(C), hid, hb.reshape(C), out, ob.reshape(C),
     )
 
 
 def solution(mesh):
-    in_specs = (P("lat", "lon", None), P("lat", "lon", None)) + (P(),) * 9
-    out_specs = (P("lat", "lon", None),) + (P(),) * 7
-    return jax.shard_map(shards, mesh=mesh, in_specs=in_specs, out_specs=out_specs, check_vma=False)
+    split = Mesh(mesh.devices.reshape(8, 2, 2, 4, 2), ("z", "x_high", "core", "y", "x_low"))
+    grid = P(LAT, LON, None)
+    in_specs = (grid, grid) + (P(),) * 9
+    out_specs = (grid,) + (P(),) * 7
+    return jax.shard_map(shards, mesh=split, in_specs=in_specs, out_specs=out_specs, check_vma=False)

time: 116 us -> 94.3 us (0.81); the launches traced: 115 us -> 94.5 us
  blocking collectives: 53.9 us -> 27.9 us
  starting transfers between devices: 9.07 us -> 23 us
  waiting for transfers between devices: 18.4 us -> 10.2 us
  Pallas kernels: 21.7 us -> 24.3 us
  other arithmetic: 4.32 us -> 1.82 us
    all_to_all x4 -> x2, blocking collectives: 53.9 us -> 27.9 us  [spread(): return lax.all_to_all(block, axis, 0, 0, tiled=True)]
    ppermute x4 -> x9, starting transfers between devices: 9.07 us -> 23 us  [swap(): return lax.ppermute(block, axis, pairs)]
    pallas_call x0 -> x2, Pallas kernels: none -> 8.39 us  [the longest x1 6.94 us: network_pass(): pl.pallas_call(network_body, out_shape=(jax.ShapeDtypeStruct((2, SLOTS *...]
    ppermute x4 -> x9, waiting for transfers between devices: 18.4 us -> 10.2 us  [swap(): return lax.ppermute(block, axis, pairs)]
    pallas_call x1, Pallas kernels: 21.7 us -> 15.9 us  [local_pass(): pl.pallas_call(body, out_shape=(jax.ShapeDtypeStruct((ROWS * COLS, C), bf...]
    unnamed x16 -> x26, local copies, waits for them, and re-layouts: 2.1 us -> 5.42 us
    slice x2 -> x0, local copies, waits for them, and re-layouts: 1.78 us -> none  [the longest x1 0.89 us: shards(): summed[:, 2 * C:3 * C]]
  transfers between devices with their start and end apart: 4 -> 9, of which waited for: 4 -> 6; matrix products, arithmetic and copies ran while one was open for 1% -> 1% of each run, Pallas kernels for 0% -> 7%
where the time goes in v2:
time: 94.3 us; the launch traced here: 94.5 us
  blocking collectives  27.9 us (30%)
  Pallas kernels  24.3 us (26%)
  starting transfers between devices  23 us (24%)
  waiting for transfers between devices  10.2 us (11%)
  local copies, waits for them, and re-layouts  5.44 us (6%)
  other arithmetic  1.82 us (2%)
  matrix products  1.03 us (1%)
    all_to_all x2, blocking collectives, spread(): return lax.all_to_all(block, axis, 0, 0, tiled=True)  27.9 us
    ppermute x9, starting transfers between devices, swap(): return lax.ppermute(block, axis, pairs)  23 us
    pallas_call x1, Pallas kernels, local_pass(): pl.pallas_call(body, out_shape=(jax.ShapeDtypeStruct((ROWS * COLS, C), bf...  15.9 us
    ppermute x9, waiting for transfers between devices, swap(): return lax.ppermute(block, axis, pairs)  10.2 us
    pallas_call x1, Pallas kernels, network_pass(): pl.pallas_call(network_body, out_shape=(jax.ShapeDtypeStruct((2, SLOTS *...  6.94 us
    unnamed x26, local copies, waits for them, and re-layouts  5.42 us
  transfers between devices with their start and end apart: 9, of which 6 were waited for; matrix products, arithmetic and copies ran while one was open for 1% of the time, Pallas kernels for 7%

profile of v2, /device:TPU:1, one launch (start us, length us, event | category | flops | bytes accessed | tf_op | source)
XLA Modules:
  0.0 94.5 jit_solution(5065241547383643529)
XLA Ops:
  0.6 0.9 copy-done
  1.5 1.0 %convolution_convert_fusion = bf16[128,256]{1,0:T(8,128)(2,1)S(1)} fusion(bf16[128,256]{1,0:T(8,128)(2,1)} %bitcast.24, bf16[256,256]{1,0:T(8,128)(2,1)S(1)} %copy-done), kind=kOutput, calls=%fused_computation | convolution fusion | flops 16809984 | bytes 262144 | tf_op jit(solution)/shard_map/dot_general | solution.py:501
  2.6 0.9 fusion.1
  3.4 2.1 %collective-permute-start = (bf16[2,4,32,256]{3,2,1,0:T(8,128)(2,1)S(1)}, bf16[2,4,32,256]{3,2,1,0:T(8,128)(2,1)S(1)}, u32[]{:S(2)}, u32[]{:S(2)}) collective-permute-start(bf16[2,4,32,256]{3,2,1,0:T(8,128)(2,1)S(1)} %get-tuple-element.45), channel_id=1, source_target_pairs={{0,1},{1,0},{2,3},{3,2},{4,5},{5,4},{6,7},{7,6},{8,9},{9,8},{10,11... | collective-permute-start | bytes 393224 | tf_op jit(solution)/shard_map/ppermute | solution.py:468
  6.3 0.7 pad_maximum_fusion.2.vec_ref
  7.0 0.9 collective-permute-done
  8.0 5.1 %collective-permute-start.3 = (bf16[3,2,4,32,256]{4,3,2,1,0:T(8,128)(2,1)S(1)}, bf16[3,2,4,32,256]{4,3,2,1,0:T(8,128)(2,1)S(1)}, u32[]{:S(2)}, u32[]{:S(2)}) collective-permute-start(bf16[3,2,4,32,256]{4,3,2,1,0:T(8,128)(2,1)S(1)} %pad_maximum_fusion.here_ref), channel_id=1, source_target_pairs={{0,248},{8,16},{16,8},{24,32},{32,24},{40,48},{48,40},{56,64},{64,... | collective-permute-start | bytes 1179656 | tf_op jit(solution)/shard_map/ppermute | solution.py:468
  13.1 4.3 %collective-permute-start.2 = (bf16[3,2,4,32,256]{4,3,2,1,0:T(8,128)(2,1)S(1)}, bf16[3,2,4,32,256]{4,3,2,1,0:T(8,128)(2,1)S(1)}, u32[]{:S(2)}, u32[]{:S(2)}) collective-permute-start(bf16[3,2,4,32,256]{4,3,2,1,0:T(8,128)(2,1)S(1)} %pad_maximum_fusion.here_ref), channel_id=1, source_target_pairs={{0,8},{8,0},{16,24},{24,16},{32,40},{40,32},{48,56},{56,48},{64,72... | collective-permute-start | bytes 1179656 | tf_op jit(solution)/shard_map/ppermute | solution.py:468
  17.4 0.9 copy-done.2
  18.3 0.9 copy-done.4
  19.2 0.7 copy-done.6
  21.8 6.9 %network_pass.1 = (f32[2,4032,128]{2,1,0:T(8,128)S(1)}, bf16[9,288,256]{2,1,0:T(8,128)(2,1)S(1)}, bf16[9,288,256]{2,1,0:T(8,128)(2,1)S(1)}, f32[9,288,256]{2,1,0...) custom-call(s32[3]{0:T(128)S(1)} %pad_add_fusion.place_ref, ...), custom_call_target="tpu_custom_call" | custom-call | flops 6000000000 | bytes 16000000 | tf_op jit(solution)/shard_map/network_pass/pallas_call | solution.py:190
  28.9 15.9 %local_pass.1 = (bf16[128,256]{1,0:T(8,128)(2,1)}, bf16[128,896]{1,0:T(8,128)(2,1)S(1)}, bf16[128,896]{1,0:T(8,128)(2,1)S(1)}) custom-call(s32[3]{0:T(128)S(1)} %pad_add_fusion.place_ref, s32[32]{0:T(128)S(1)} %copy-done.8, s32[32]{0:T(128)S(1)} %copy-done.10, f32[4,64]{1,0:T(4,128)S(1)} %copy-done.12, ...), custom_call_target="tpu_custom_call" | custom-call | flops 8999999488 | bytes 24000000 | tf_op jit(solution)/shard_map/local_pass/pallas_call | solution.py:434
  44.7 1.5 %collective-permute-done.4 = bf16[128,896]{1,0:T(8,128)(2,1)S(1)} collective-permute-done((bf16[128,896]{1,0:T(8,128)(2,1)S(1)}, bf16[128,896]{1,0:T(8,128)(2,1)S(1)}, u32[]{:S(2)}, u32[]{:S(2)}) %collective-permute-start.4) | collective-permute-done | bytes 229408 | tf_op jit(solution)/shard_map/ppermute | solution.py:468
  46.3 17.5 %all_to_all.10 = bf16[16,8,896]{2,1,0:T(8,128)(2,1)S(1)} all-to-all(bf16[16,8,896]{2,1,0:T(8,128)(2,1)S(1)} %fusion), channel_id=1, replica_groups=mesh['z'=8,'x_high'=2,'core'=2,'y'=4,'x_low'=2] {'y','x_low','x_high'}, dimensions={0} | all-to-all | bytes 458752 | tf_op jit(solution)/shard_map/all_to_all | solution.py:479
  63.9 2.7 %collective-permute-done.5 = f32[8,896]{1,0:T(8,128)S(1)} collective-permute-done((f32[8,896]{1,0:T(8,128)S(1)}, f32[8,896]{1,0:T(8,128)S(1)}, u32[]{:S(2)}, u32[]{:S(2)}) %collective-permute-start.5) | collective-permute-done | bytes 28704 | tf_op jit(solution)/shard_map/ppermute | solution.py:468
  66.6 1.9 %collective-permute-start.6 = (f32[8,896]{1,0:T(8,128)S(1)}, f32[8,896]{1,0:T(8,128)S(1)}, u32[]{:S(2)}, u32[]{:S(2)}) collective-permute-start(f32[8,896]{1,0:T(8,128)S(1)} %add.22), channel_id=1, source_target_pairs={{0,64},{32,96},{64,0},{96,32},{128,192},{160,224},{192,128},{224,1... | collective-permute-start | bytes 86024 | tf_op jit(solution)/shard_map/ppermute | solution.py:468
  68.5 1.7 %collective-permute-done.6 = f32[8,896]{1,0:T(8,128)S(1)} collective-permute-done((f32[8,896]{1,0:T(8,128)S(1)}, f32[8,896]{1,0:T(8,128)S(1)}, u32[]{:S(2)}, u32[]{:S(2)}) %collective-permute-start.6) | collective-permute-done | bytes 28704 | tf_op jit(solution)/shard_map/ppermute | solution.py:468
  70.3 2.6 %collective-permute-start.7 = (f32[8,896]{1,0:T(8,128)S(1)}, f32[8,896]{1,0:T(8,128)S(1)}, u32[]{:S(2)}, u32[]{:S(2)}) collective-permute-start(f32[8,896]{1,0:T(8,128)S(1)} %add.23), channel_id=1, source_target_pairs={{0,192},{32,224},{64,128},{96,160},{128,64},{160,96},{192,0},{224,... | collective-permute-start | bytes 86024 | tf_op jit(solution)/shard_map/ppermute | solution.py:468
  72.9 2.3 %collective-permute-done.7 = f32[8,896]{1,0:T(8,128)S(1)} collective-permute-done((f32[8,896]{1,0:T(8,128)S(1)}, f32[8,896]{1,0:T(8,128)S(1)}, u32[]{:S(2)}, u32[]{:S(2)}) %collective-permute-start.7) | collective-permute-done | bytes 28704 | tf_op jit(solution)/shard_map/ppermute | solution.py:468
  75.2 10.4 %all_to_all.11 = bf16[16,8,896]{2,1,0:T(8,128)(2,1)S(1)} all-to-all(bf16[16,8,896]{2,1,0:T(8,128)(2,1)S(1)} %broadcast_in_dim.2), channel_id=1, replica_groups=mesh['z'=8,'x_high'=2,'core'=2,'y'=4,'x_low'=2] {'y','x_low','x_high'}, dimensions={0} | all-to-all | bytes 458752 | tf_op jit(solution)/shard_map/all_to_all | solution.py:479
  85.7 6.3 %collective-permute-start.8 = (bf16[128,896]{1,0:T(8,128)(2,1)S(1)}, bf16[128,896]{1,0:T(8,128)(2,1)S(1)}, u32[]{:S(2)}, u32[]{:S(2)}) collective-permute-start(bf16[128,896]{1,0:T(8,128)(2,1)S(1)} %bitcast.22), channel_id=1, source_target_pairs={{0,8},{8,0},{1,9},{9,1},{2,10},{10,2},{3,11},{11,3},{4,12},{12,4},... | collective-permute-start | bytes 688136 | tf_op jit(solution)/shard_map/ppermute | solution.py:468
  92.0 1.1 %collective-permute-done.8.other_ref = bf16[128,896]{1,0:T(8,128)(2,1)S(1)} collective-permute-done((bf16[128,896]{1,0:T(8,128)(2,1)S(1)}, bf16[128,896]{1,0:T(8,128)(2,1)S(1)}, u32[]{:S(2)}, u32[]{:S(2)}) %collective-permute-start.8) | collective-permute-done | bytes 229408 | tf_op jit(solution)/shard_map/ppermute | solution.py:468
  93.1 1.4 %unpack.1 = (f32[256,256]{1,0:T(8,128)}, f32[256,256]{1,0:T(8,128)}, f32[256,256]{1,0:T(8,128)}, f32[3,256]{1,0:T(4,128)}, f32[1,256]{1,0:T(1,128)}, /*index=5*/f32[1,256]{1,0:T(1,128)}, f32[1,256]{1,0:T(1,128)}) custom-call(s32[3]{0:T(128)S(1)} %pad_add_fusion.place_ref, bf16[128,896]{1,0:T(8,128)(2,1)S(1)} %bitcast.23, ...), custom_call_target="tpu_custom_call" | custom-call | tf_op jit(solution)/shard_map/unpack/pallas_call | solution.py:420
  (36 shorter events, 3.1 us)
Async XLA Ops:
  0.6 0.9 copy-start
  3.4 4.5 %collective-permute-start = (bf16[2,4,32,256]{3,2,1,0:T(8,128)(2,1)S(1)}, bf16[2,4,32,256]{3,2,1,0:T(8,128)(2,1)S(1)}, u32[]{:S(2)}, u32[]{:S(2)}) collective-permute-start(bf16[2,4,32,256]{3,2,1,0:T(8,128)(2,1)S(1)} %get-tuple-element.45), channel_id=1, source_target_pairs={{0,1},{1,0},{2,3},{3,2},{4,5},{5,4},{6,7},{7,6},{8,9},{9,8},{10,11... | collective-permute-start | bytes 393224 | tf_op jit(solution)/shard_map/ppermute | solution.py:468
  5.6 2.4 %collective-permute-start.1 = (bf16[2,4,32,256]{3,2,1,0:T(8,128)(2,1)S(1)}, bf16[2,4,32,256]{3,2,1,0:T(8,128)(2,1)S(1)}, u32[]{:S(2)}, u32[]{:S(2)}) collective-permute-start(bf16[2,4,32,256]{3,2,1,0:T(8,128)(2,1)S(1)} %get-tuple-element.45), channel_id=1, source_target_pairs={{1,2},{2,1},{3,4},{4,3},{5,6},{6,5},{9,10},{10,9},{11,12},{12,11},... | collective-permute-start | bytes 393224 | tf_op jit(solution)/shard_map/ppermute | solution.py:468
  7.9 20.9 %copy-start.3 = (bf16[256,256]{1,0:T(8,128)(2,1)S(1)}, bf16[256,256]{1,0:T(8,128)(2,1)}, u32[]{:S(2)}) copy-start(bf16[256,256]{1,0:T(8,128)(2,1)} %hw_ref.3) | copy-start | bytes 393220
  7.9 20.9 %copy-start.5 = (bf16[256,256]{1,0:T(8,128)(2,1)S(1)}, bf16[256,256]{1,0:T(8,128)(2,1)}, u32[]{:S(2)}) copy-start(bf16[256,256]{1,0:T(8,128)(2,1)} %ow_ref.3) | copy-start | bytes 393220
  7.9 20.9 %copy-start.8 = (s32[32]{0:T(128)S(1)}, s32[32]{0:T(128)}, u32[]{:S(2)}) copy-start(s32[32]{0:T(128)} %lon_ref.3) | copy-start | bytes 388
  7.9 20.9 %copy-start.10 = (s32[32]{0:T(128)S(1)}, s32[32]{0:T(128)}, u32[]{:S(2)}) copy-start(s32[32]{0:T(128)} %lat_ref.3) | copy-start | bytes 388
  7.9 20.9 %copy-start.12 = (f32[4,64]{1,0:T(4,128)S(1)}, f32[4,64]{1,0:T(4,128)}, u32[]{:S(2)}) copy-start(f32[4,64]{1,0:T(4,128)} %constant.30.clone.tab_ref) | copy-start | bytes 3076
  8.0 20.9 %copy-start.1 = (bf16[4,32,256]{2,1,0:T(8,128)(2,1)S(1)}, bf16[4,32,256]{2,1,0:T(8,128)(2,1)}, u32[]{:S(2)}) copy-start(bf16[4,32,256]{2,1,0:T(8,128)(2,1)} %param.14) | copy-start | bytes 196612
  8.0 20.8 %collective-permute-start.3 = (bf16[3,2,4,32,256]{4,3,2,1,0:T(8,128)(2,1)S(1)}, bf16[3,2,4,32,256]{4,3,2,1,0:T(8,128)(2,1)S(1)}, u32[]{:S(2)}, u32[]{:S(2)}) collective-permute-start(bf16[3,2,4,32,256]{4,3,2,1,0:T(8,128)(2,1)S(1)} %pad_maximum_fusion.here_ref), channel_id=1, source_target_pairs={{0,248},{8,16},{16,8},{24,32},{32,24},{40,48},{48,40},{56,64},{64,... | collective-permute-start | bytes 1179656 | tf_op jit(solution)/shard_map/ppermute | solution.py:468
  13.1 15.7 %collective-permute-start.2 = (bf16[3,2,4,32,256]{4,3,2,1,0:T(8,128)(2,1)S(1)}, bf16[3,2,4,32,256]{4,3,2,1,0:T(8,128)(2,1)S(1)}, u32[]{:S(2)}, u32[]{:S(2)}) collective-permute-start(bf16[3,2,4,32,256]{4,3,2,1,0:T(8,128)(2,1)S(1)} %pad_maximum_fusion.here_ref), channel_id=1, source_target_pairs={{0,8},{8,0},{16,24},{24,16},{32,40},{40,32},{48,56},{56,48},{64,72... | collective-permute-start | bytes 1179656 | tf_op jit(solution)/shard_map/ppermute | solution.py:468
  17.4 0.9 copy-start.2
  18.3 0.9 copy-start.4
  19.2 0.7 copy-start.6
  19.9 0.7 copy-start.7
  20.5 0.7 copy-start.9
  21.2 0.7 copy-start.11
  44.7 1.5 %collective-permute-start.4 = (bf16[128,896]{1,0:T(8,128)(2,1)S(1)}, bf16[128,896]{1,0:T(8,128)(2,1)S(1)}, u32[]{:S(2)}, u32[]{:S(2)}) collective-permute-start(bf16[128,896]{1,0:T(8,128)(2,1)S(1)} %get-tuple-element.36), channel_id=1, source_target_pairs={{0,8},{8,0},{1,9},{9,1},{2,10},{10,2},{3,11},{11,3},{4,12},{12,4},... | collective-permute-start | bytes 688136 | tf_op jit(solution)/shard_map/ppermute | solution.py:468
  63.8 2.8 %collective-permute-start.5 = (f32[8,896]{1,0:T(8,128)S(1)}, f32[8,896]{1,0:T(8,128)S(1)}, u32[]{:S(2)}, u32[]{:S(2)}) collective-permute-start(f32[8,896]{1,0:T(8,128)S(1)} %convert_reduce_fusion), channel_id=1, source_target_pairs={{0,32},{32,0},{64,96},{96,64},{128,160},{160,128},{192,224},{224,1... | collective-permute-start | bytes 86024 | tf_op jit(solution)/shard_map/ppermute | solution.py:468
  66.6 3.6 %collective-permute-start.6 = (f32[8,896]{1,0:T(8,128)S(1)}, f32[8,896]{1,0:T(8,128)S(1)}, u32[]{:S(2)}, u32[]{:S(2)}) collective-permute-start(f32[8,896]{1,0:T(8,128)S(1)} %add.22), channel_id=1, source_target_pairs={{0,64},{32,96},{64,0},{96,32},{128,192},{160,224},{192,128},{224,1... | collective-permute-start | bytes 86024 | tf_op jit(solution)/shard_map/ppermute | solution.py:468
  70.3 4.9 %collective-permute-start.7 = (f32[8,896]{1,0:T(8,128)S(1)}, f32[8,896]{1,0:T(8,128)S(1)}, u32[]{:S(2)}, u32[]{:S(2)}) collective-permute-start(f32[8,896]{1,0:T(8,128)S(1)} %add.23), channel_id=1, source_target_pairs={{0,192},{32,224},{64,128},{96,160},{128,64},{160,96},{192,0},{224,... | collective-permute-start | bytes 86024 | tf_op jit(solution)/shard_map/ppermute | solution.py:468
  85.7 7.4 %collective-permute-start.8 = (bf16[128,896]{1,0:T(8,128)(2,1)S(1)}, bf16[128,896]{1,0:T(8,128)(2,1)S(1)}, u32[]{:S(2)}, u32[]{:S(2)}) collective-permute-start(bf16[128,896]{1,0:T(8,128)(2,1)S(1)} %bitcast.22), channel_id=1, source_target_pairs={{0,8},{8,0},{1,9},{9,1},{2,10},{10,2},{3,11},{11,3},{4,12},{12,4},... | collective-permute-start | bytes 688136 | tf_op jit(solution)/shard_map/ppermute | solution.py:468

commit v3 on v2

v3 whole, which is shorter than its diff:
```python
import functools
import math

import jax
import jax.numpy as jnp
import numpy as np
from jax import lax
from jax.experimental import pallas as pl
from jax.experimental.pallas import tpu as pltpu
from jax.sharding import Mesh
from jax.sharding import PartitionSpec as P

HLON = 32
HLAT = 4
NLAT = 32
NLON = 1024
ROWS = 4
COLS = 32
EXT = ROWS + 2 * HLAT
C = 256
HALF = 128
TAPS = 72
TLAT = 2 * HLAT + 1
GROUP = 4
SPAN = GROUP * TAPS
SLOTS = 56
OWN = ROWS * TLAT
WIN = 76
PAIRS = 40
HEAD = 3
LINE = 104
PACK = 3 * C + HALF
MAGIC = 12582912.0
TURN = 1.0 / (2.0 * math.pi)

f32 = jnp.float32
bf16 = jnp.bfloat16

SIN_POLY = (0.99999995, -19.73917132, 64.93458165, -85.24010036, 56.24054044)
COS_POLY = (6.28318528, -41.34168067, 81.60248074, -76.58128456, 39.76072208)


def tables(lon_half, lat_half):
    lon, lat = lon_half.astype(f32), lat_half.astype(f32)
    sine = jnp.asarray(np.sin(np.pi * ((np.arange(NLAT) + 0.5) / NLAT - 0.5)).astype(np.float32))
    return jnp.stack((1.0 / lon, 1.0 / lat, lax.rsqrt((2.0 * lon + 1.0) * (2.0 * lat + 1.0)), sine))


def horner(u, poly):
    total = poly[-1] * u + poly[-2]
    for c in poly[-3::-1]:
        total = total * u + c
    return total


def sine_cosine(turns):
    part = turns - ((turns + MAGIC) - MAGIC)
    h = jnp.abs(part) - 0.25
    u = h * h
    s = horner(u, SIN_POLY)
    return jnp.where(part < 0, -s, s), -h * horner(u, COS_POLY)


def reduce_eight(parts, masks):
    for shift, mask in zip((1, 2, 4), masks):
        merged = []
        for i in range(0, len(parts), 2):
            x, y = parts[i], parts[i + 1]
            merged.append(jnp.where(mask, x, y) + pltpu.roll(jnp.where(mask, y, x), 8 - shift, 0))
        parts = merged
    return parts[0]


def lon_of(place_ref, i):
    return place_ref[HEAD + i]


def lat_of(place_ref, i):
    return place_ref[HEAD + NLAT + i]


def grid_row(place_ref, e):
    return place_ref[0] + e - HLAT


def in_grid(place_ref, e):
    i = grid_row(place_ref, e)
    return jnp.logical_and(i >= 0, i < NLAT)


def safe_row(place_ref, e):
    return jnp.clip(grid_row(place_ref, e), 0, NLAT - 1)


def number_slots(place_ref, slot_row, slot_tap, first_slot, low_tap, high_tap):
    def add_slots(e, lo, hi, count):
        low_tap[e] = lo
        high_tap[e] = hi
        first_slot[e] = count - lo

        def add(a, n):
            slot_row[n] = e
            slot_tap[n] = a
            return n + 1

        return lax.fori_loop(lo, hi + 1, add, count)

    def own_slots(r, count):
        e = r + HLAT
        i = grid_row(place_ref, e)
        h = lat_of(place_ref, i)
        return add_slots(e, jnp.maximum(-h, -i), jnp.minimum(h, NLAT - 1 - i), count)

    own_count = lax.fori_loop(0, ROWS, own_slots, 0)

    def edge_slots(t, count):
        e = jnp.where(t < HLAT, t, t + ROWS)
        h = lat_of(place_ref, safe_row(place_ref, e))
        lo = jnp.maximum(-h, HLAT - e)
        hi = jnp.minimum(h, HLAT + ROWS - 1 - e)
        hi = jnp.where(in_grid(place_ref, e), hi, lo - 1)
        return add_slots(e, lo, hi, count)

    return own_count, lax.fori_loop(0, 2 * HLAT, edge_slots, own_count)


def lay_taps(g, taps, kern, ksum):
    wide = taps.astype(f32)
    at = pl.multiple_of(g * SPAN, 8)
    kern[0, pl.ds(at, SPAN), :] = wide[:, :HALF]
    kern[1, pl.ds(at, SPAN), :] = wide[:, HALF:]
    for q in range(GROUP):
        to = pl.multiple_of((GROUP * g + q) * PAIRS, 8)
        for h in range(2):
            even = kern[h, pl.ds(at + q * TAPS, PAIRS - 4, stride=2), :]
            odd = kern[h, pl.ds(at + q * TAPS + 1, PAIRS - 4, stride=2), :]
            ksum[h, pl.ds(to, PAIRS - 4), :] = even + odd


def network_body(
    place_ref, tab_ref, vec_ref, weight_ref,
    kern, ksum, packed, h1_ref, h2_ref, c2_ref, own_sin_lon, own_cos_lon, own_sin_lat, own_cos_lat,
    slot_row, slot_tap, first_slot, low_tap, high_tap, sin_lon, cos_lon, sin_lat, cos_lat,
):
    own_count, slot_count = number_slots(place_ref, slot_row, slot_tap, first_slot, low_tap, high_tap)
    own_groups = (own_count + GROUP - 1) // GROUP
    tap_index = lax.broadcasted_iota(jnp.int32, (TAPS, C), 0)
    lat_index = (lax.broadcasted_iota(jnp.int32, (16, C), 0) - HLAT).astype(f32)
    fw = vec_ref[0:3]
    first_bias = vec_ref[3:4]
    hidden_bias = vec_ref[4:5] * TURN
    output_bias = vec_ref[5:6]
    omega = 30.0 * TURN

    def angles(e, _):
        @pl.when(in_grid(place_ref, e))
        def _():
            i = safe_row(place_ref, e)
            w = lon_of(place_ref, i)
            lon = (tap_index - w).astype(f32) * tab_ref[0, i]
            phase = (lon * fw[0:1] + (tab_ref[3, i] * fw[2:3] + first_bias)) * omega
            s, c = sine_cosine(phase)
            sin_lon[e] = s
            cos_lon[e] = c
            s, c = sine_cosine((lat_index * tab_ref[1, i]) * fw[1:2] * omega)
            sin_lat[e] = s
            cos_lat[e] = c

        return 0

    lax.fori_loop(0, EXT, angles, 0)

    def network(g, _):
        pos = [jnp.minimum(GROUP * g + q, slot_count - 1) for q in range(GROUP)]
        rows = [slot_row[n] for n in pos]
        hidden = []
        for n, e in zip(pos, rows):
            t = slot_tap[n] + HLAT
            hidden.append(sin_lon[e] * cos_lat[e, pl.ds(t, 1), :] + cos_lon[e] * sin_lat[e, pl.ds(t, 1), :])
        h1 = jnp.concatenate(hidden, axis=0).astype(bf16)
        pre = jnp.dot(h1, weight_ref[0], preferred_element_type=f32) * TURN + hidden_bias
        s, c = sine_cosine(pre)
        h2 = s.astype(bf16)

        @pl.when(g < own_groups)
        def _():
            h1_ref[g] = h1
            h2_ref[g] = h2
            c2_ref[g] = c

        raw = jnp.dot(h2, weight_ref[1], preferred_element_type=f32) + output_bias
        taps = []
        for q in range(GROUP):
            i = safe_row(place_ref, rows[q])
            limit = 2 * lon_of(place_ref, i)
            taps.append(jnp.where(tap_index <= limit, raw[q * TAPS:(q + 1) * TAPS] * tab_ref[2, i], 0.0))
        taps = jnp.concatenate(taps, axis=0).astype(bf16)
        packed[g] = taps
        lay_taps(g, taps, kern, ksum)
        return 0

    lax.fori_loop(0, (slot_count + GROUP - 1) // GROUP, network, 0)
    for own, every in (
        (own_sin_lon, sin_lon), (own_cos_lon, cos_lon), (own_sin_lat, sin_lat), (own_cos_lat, cos_lat),
    ):
        own[...] = every[HLAT:HLAT + ROWS]


def network_pass(place, table, vectors, weights):
    smem = pl.BlockSpec(memory_space=pltpu.SMEM)
    vmem = pl.BlockSpec(memory_space=pltpu.VMEM)
    return pl.pallas_call(
        network_body,
        out_shape=(
            jax.ShapeDtypeStruct((2, SLOTS * TAPS, HALF), f32),
            jax.ShapeDtypeStruct((2, SLOTS * PAIRS, HALF), f32),
            jax.ShapeDtypeStruct((SLOTS // GROUP, SPAN, C), bf16),
            jax.ShapeDtypeStruct((OWN // GROUP, SPAN, C), bf16),
            jax.ShapeDtypeStruct((OWN // GROUP, SPAN, C), bf16),
            jax.ShapeDtypeStruct((OWN // GROUP, SPAN, C), f32),
            jax.ShapeDtypeStruct((ROWS, TAPS, C), f32),
            jax.ShapeDtypeStruct((ROWS, TAPS, C), f32),
            jax.ShapeDtypeStruct((ROWS, 16, C), f32),
            jax.ShapeDtypeStruct((ROWS, 16, C), f32),
        ),
        in_specs=[smem] * 2 + [vmem] * 2,
        out_specs=(vmem,) * 10,
        scratch_shapes=[
            pltpu.SMEM((SLOTS + 8,), jnp.int32),
            pltpu.SMEM((SLOTS + 8,), jnp.int32),
            pltpu.SMEM((16,), jnp.int32),
            pltpu.SMEM((16,), jnp.int32),
            pltpu.SMEM((16,), jnp.int32),
            pltpu.VMEM((EXT, TAPS, C), f32),
            pltpu.VMEM((EXT, TAPS, C), f32),
            pltpu.VMEM((EXT, 16, C), f32),
            pltpu.VMEM((EXT, 16, C), f32),
        ],
        compiler_params=pltpu.CompilerParams(vmem_limit_bytes=16 * 1024 * 1024),
        cost_estimate=pl.CostEstimate(flops=6_000_000_000, bytes_accessed=16_000_000, transcendentals=0),
        name="network_pass",
    )(place, table, vectors, weights)


def build_windows(place_ref, here_ref, inner_ref, outer_ref, which, front, line, window, change):
    lat_odd = place_ref[2] == 1
    left_inner = place_ref[1] == 1

    def one(e, _):
        @pl.when(in_grid(place_ref, e))
        def _():
            band = e // ROWS
            part = jnp.where(band == 1, 0, jnp.where((band == 2) == lat_odd, 2, 1))
            row = e % ROWS
            for n in range(2):
                lanes = slice(n * HALF, (n + 1) * HALF)
                near = inner_ref[part, which, row, :, lanes].astype(f32)
                far = outer_ref[part, which, row, :, lanes].astype(f32)
                line[n, 0:8] = jnp.zeros((8, HALF), f32)
                line[n, 96:LINE] = jnp.zeros((LINE - 96, HALF), f32)
                line[n, front:front + 32] = jnp.where(left_inner, near, far)
                line[n, front + 32:front + 64] = here_ref[part, which, row, :, lanes].astype(f32)
                line[n, front + 64:front + 96] = jnp.where(left_inner, far, near)
            for n in range(2):
                last = None
                for p in range(WIN):
                    value = line[n, pl.ds(p, 8, stride=4), :]
                    window[e, n, p] = value
                    if p:
                        change[e, n, p - 1] = last - value
                    last = value

        return 0

    lax.fori_loop(0, EXT, one, 0)


def taps_of(window, change, e, n, start):
    odd = [window[e, n, start + 2 * i + 1] for i in range(5)]
    fall = [change[e, n, start + 2 * i] for i in range(5)]
    next_fall = [change[e, n, start + 2 * i + 1] for i in range(5)]
    return odd, fall, next_fall


def row_of(source, h, at):
    return source[h, pl.ds(at, 8, stride=0), :]


def combine(total):
    p0, p1, q0, q1, r0, r1 = total
    return p0 + q0, p0 - r0, p1 + q1, p1 - r1


def gradient_body(
    place_ref, tab_ref, here_ref, inner_ref, outer_ref, cot_ref, weight_ref,
    kern, ksum, h1_ref, h2_ref, c2_ref, sin_lon, cos_lon, sin_lat, cos_lat,
    keep_ref, send_ref,
    slot_row, slot_tap, first_slot, low_tap, high_tap,
    line, window, change, mine_line, grad, conv, d_mix, d_out, d_hid, d_small, d_side,
):
    inverse = 1.0 / math.sqrt(NLAT * NLON)
    own_count, slot_count = number_slots(place_ref, slot_row, slot_tap, first_slot, low_tap, high_tap)
    tap_index = lax.broadcasted_iota(jnp.int32, (TAPS, C), 0)
    core = place_ref[1]
    for h in range(2):
        mine_line[h] = here_ref[0, 1, :, :, h * HALF:(h + 1) * HALF].reshape(ROWS * COLS, HALF).astype(f32)
    build_windows(place_ref, here_ref, inner_ref, outer_ref, 0, 0, line, window, change)
    sub = lax.broadcasted_iota(jnp.int32, (8, HALF), 0)
    masks = [(sub & bit) == 0 for bit in (1, 2, 4)]
    zero = jnp.zeros((8, HALF), f32)

    def conv_row(r, _):
        e = r + HLAT
        w = lon_of(place_ref, grid_row(place_ref, e))
        blocks = (2 * w + 8) // 8
        mine = [[mine_line[h, pl.ds(r * COLS + t, 8, stride=4), :] for t in range(4)] for h in range(2)]
        both = [[m[0] + m[1], m[2] + m[3]] for m in mine]

        def one_lat(a, total):
            slot = first_slot[e] + a

            def one_block(b, total):
                new = []
                start = HLON - w + 8 * b
                at = slot * TAPS + 8 * b
                pair = slot * PAIRS + 4 * b
                for h in range(2):
                    acc = list(total[6 * h:6 * h + 6])
                    odd, fall, next_fall = taps_of(window, change, e + a, h, start)
                    parts = []
                    for j in range(4):
                        k_sum = row_of(ksum, h, pair + j)
                        k_even = row_of(kern, h, at + 2 * j)
                        k_odd = row_of(kern, h, at + 2 * j + 1)
                        for m in range(2):
                            acc[m] = acc[m] + k_sum * odd[m + j]
                            acc[2 + m] = acc[2 + m] + k_even * fall[m + j]
                            acc[4 + m] = acc[4 + m] + k_odd * next_fall[m + j]
                        p = both[h][0] * odd[j] + both[h][1] * odd[j + 1]
                        parts.append(p + (mine[h][0] * fall[j] + mine[h][2] * fall[j + 1]))
                        parts.append(p - (mine[h][1] * next_fall[j] + mine[h][3] * next_fall[j + 1]))
                    grad[h, pl.ds(pl.multiple_of(at, 8), 8), :] = reduce_eight(parts, masks)
                    new += acc
                return tuple(new)

            return lax.fori_loop(0, blocks, one_block, total)

        total = lax.fori_loop(low_tap[e], high_tap[e] + 1, one_lat, (zero,) * 12)
        for h in range(2):
            for t, value in enumerate(combine(total[6 * h:6 * h + 6])):
                conv[h, pl.ds(r * COLS + t, 8, stride=4), :] = value
        return 0

    lax.fori_loop(0, ROWS, conv_row, 0)
    for h in range(2):
        d_mix[h * HALF:(h + 1) * HALF, :] = lax.dot_general(
            conv[h].astype(bf16), cot_ref[...], (((0,), (0,)), ((), ())), preferred_element_type=f32
        )

    d_out[...] = jnp.zeros_like(d_out)
    d_hid[...] = jnp.zeros_like(d_hid)
    d_small[...] = jnp.zeros_like(d_small)

    def adjoint(g, _):
        raw = []
        pos = [jnp.minimum(GROUP * g + q, own_count - 1) for q in range(GROUP)]
        rows = [slot_row[n] for n in pos]
        for q in range(GROUP):
            i = grid_row(place_ref, rows[q])
            w = lon_of(place_ref, i)
            norm = tab_ref[2, i]
            limit = jnp.where(GROUP * g + q < own_count, 2 * w, -1)
            at = pl.multiple_of(pos[q] * TAPS, 8)
            part = jnp.concatenate([grad[0, pl.ds(at, TAPS), :], grad[1, pl.ds(at, TAPS), :]], axis=1)
            raw.append(jnp.where(tap_index <= limit, part * norm, 0.0))
        raw = jnp.concatenate(raw, axis=0)
        raw_low = raw.astype(bf16)
        h1 = h1_ref[g]
        h2 = h2_ref[g]
        rows_by_rows = (((0,), (0,)), ((), ()))
        d_out[...] += lax.dot_general(h2, raw_low, rows_by_rows, preferred_element_type=f32)
        d_small[5:6, :] += jnp.sum(raw, axis=0, keepdims=True)
        gp = lax.dot_general(
            raw_low, weight_ref[1], (((1,), (1,)), ((), ())), preferred_element_type=f32
        ) * c2_ref[g]
        gp_low = gp.astype(bf16)
        d_hid[...] += lax.dot_general(h1, gp_low, rows_by_rows, preferred_element_type=f32)
        d_small[4:5, :] += jnp.sum(gp, axis=0, keepdims=True)
        gf = lax.dot_general(
            gp_low, weight_ref[0], (((1,), (1,)), ((), ())), preferred_element_type=f32
        )
        for q in range(GROUP):
            e = rows[q]
            i = grid_row(place_ref, e)
            w = lon_of(place_ref, i)
            a = slot_tap[pos[q]]
            t = a + HLAT
            c1 = cos_lon[e - HLAT] * cos_lat[e - HLAT, pl.ds(t, 1), :] - sin_lon[e - HLAT] * sin_lat[e - HLAT, pl.ds(t, 1), :]
            gq = gf[q * TAPS:(q + 1) * TAPS] * c1
            lon = (tap_index - w).astype(f32) * tab_ref[0, i]
            total = jnp.sum(gq, axis=0, keepdims=True)
            d_small[0:1, :] += jnp.sum(gq * lon, axis=0, keepdims=True)
            d_small[1:2, :] += total * (a.astype(f32) * tab_ref[1, i])
            d_small[2:3, :] += total * tab_ref[3, i]
            d_small[3:4, :] += total
        return 0

    lax.fori_loop(0, (own_count + GROUP - 1) // GROUP, adjoint, 0)
    d_small[0:4, :] = d_small[0:4, :] * 30.0
    d_side[...] = jnp.transpose(d_small[...])
    for target, half in ((keep_ref, core), (send_ref, 1 - core)):
        rows = pl.ds(pl.multiple_of(half * HALF, HALF), HALF)
        for q, source in enumerate((d_mix, d_hid, d_out, d_side)):
            part = source[rows, :] * inverse
            target[:, q * C:q * C + part.shape[1]] = part.astype(bf16)


def back_body(
    place_ref, here_ref, inner_ref, outer_ref, packed, gfield_ref,
    slot_row, slot_tap, first_slot, low_tap, high_tap, line, window, change, kern, ksum, back,
):
    _, slot_count = number_slots(place_ref, slot_row, slot_tap, first_slot, low_tap, high_tap)

    def lay(g, _):
        lay_taps(g, packed[g], kern, ksum)
        return 0

    lax.fori_loop(0, (slot_count + GROUP - 1) // GROUP, lay, 0)
    build_windows(place_ref, here_ref, inner_ref, outer_ref, 1, 8, line, window, change)
    zero = jnp.zeros((8, HALF), f32)

    def back_row(r, _):
        def one_source(e, total):
            a = r + HLAT - e
            i = safe_row(place_ref, e)
            w = lon_of(place_ref, i)
            live = jnp.logical_and(in_grid(place_ref, e), jnp.abs(a) <= lat_of(place_ref, i))
            blocks = jnp.where(live, (2 * w + 8) // 8, 0)
            slot = first_slot[e] + a

            def one_block(b, total):
                start = HLON + 1 + w - 8 * b
                at = slot * TAPS + 8 * b
                pair = slot * PAIRS + 4 * b
                new = []
                for h in range(2):
                    acc = list(total[6 * h:6 * h + 6])
                    odd, fall, next_fall = taps_of(window, change, e, h, start)
                    for j in range(4):
                        k_sum = row_of(ksum, h, pair + 3 - j)
                        k_even = row_of(kern, h, at + 7 - 2 * j)
                        k_odd = row_of(kern, h, at + 6 - 2 * j)
                        for m in range(2):
                            acc[m] = acc[m] + k_sum * odd[m + j]
                            acc[2 + m] = acc[2 + m] + k_even * fall[m + j]
                            acc[4 + m] = acc[4 + m] + k_odd * next_fall[m + j]
                    new += acc
                return tuple(new)

            return lax.fori_loop(0, blocks, one_block, total)

        total = lax.fori_loop(r, r + TLAT, one_source, (zero,) * 12)
        for h in range(2):
            for t, value in enumerate(combine(total[6 * h:6 * h + 6])):
                back[h, pl.ds(r * COLS + t, 8, stride=4), :] = value
        return 0

    lax.fori_loop(0, ROWS, back_row, 0)
    for h in range(2):
        gfield_ref[:, h * HALF:(h + 1) * HALF] = back[h].astype(bf16)


def unpack_body(place_ref, own_ref, other_ref, mix_ref, hid_ref, out_ref, first_ref, fb_ref, hb_ref, ob_ref, side):
    core = place_ref[1]
    for source, half in ((own_ref, core), (other_ref, 1 - core)):
        rows = pl.ds(pl.multiple_of(half * HALF, HALF), HALF)
        for q, target in enumerate((mix_ref, hid_ref, out_ref)):
            target[rows, :] = source[:, q * C:(q + 1) * C].astype(f32)
        side[rows, :] = source[:, 3 * C:].astype(f32)
    small = jnp.transpose(side[...])
    first_ref[...] = small[0:3]
    fb_ref[...] = small[3:4]
    hb_ref[...] = small[4:5]
    ob_ref[...] = small[5:6]


def unpack(place, own, other):
    vmem = pl.BlockSpec(memory_space=pltpu.VMEM)
    square = jax.ShapeDtypeStruct((C, C), f32)
    line = jax.ShapeDtypeStruct((1, C), f32)
    return pl.pallas_call(
        unpack_body,
        out_shape=(square, square, square, jax.ShapeDtypeStruct((3, C), f32), line, line, line),
        in_specs=[pl.BlockSpec(memory_space=pltpu.SMEM)] + [vmem] * 2,
        out_specs=(vmem,) * 7,
        scratch_shapes=[pltpu.VMEM((C, HALF), f32)],
        compiler_params=pltpu.CompilerParams(vmem_limit_bytes=8 * 1024 * 1024),
        name="unpack",
    )(place, own, other)


def slot_scratch():
    return [
        pltpu.SMEM((SLOTS + 8,), jnp.int32),
        pltpu.SMEM((SLOTS + 8,), jnp.int32),
        pltpu.SMEM((16,), jnp.int32),
        pltpu.SMEM((16,), jnp.int32),
        pltpu.SMEM((16,), jnp.int32),
    ]


def gradient_pass(place, table, here, inner, outer, cotangent, weights, saved):
    smem = pl.BlockSpec(memory_space=pltpu.SMEM)
    vmem = pl.BlockSpec(memory_space=pltpu.VMEM)
    return pl.pallas_call(
        gradient_body,
        out_shape=(
            jax.ShapeDtypeStruct((C // 2, PACK), bf16),
            jax.ShapeDtypeStruct((C // 2, PACK), bf16),
        ),
        in_specs=[smem] * 2 + [vmem] * 14,
        out_specs=(vmem,) * 2,
        scratch_shapes=slot_scratch() + [
            pltpu.VMEM((2, LINE, HALF), f32),
            pltpu.VMEM((EXT, 2, WIN, 8, HALF), f32),
            pltpu.VMEM((EXT, 2, WIN, 8, HALF), f32),
            pltpu.VMEM((2, ROWS * COLS, HALF), f32),
            pltpu.VMEM((2, OWN * TAPS, HALF), f32),
            pltpu.VMEM((2, ROWS * COLS, HALF), f32),
            pltpu.VMEM((C, C), f32),
            pltpu.VMEM((C, C), f32),
            pltpu.VMEM((C, C), f32),
            pltpu.VMEM((HALF, C), f32),
            pltpu.VMEM((C, HALF), f32),
        ],
        compiler_params=pltpu.CompilerParams(vmem_limit_bytes=26 * 1024 * 1024),
        cost_estimate=pl.CostEstimate(flops=9_000_000_000, bytes_accessed=20_000_000, transcendentals=0),
        name="gradient_pass",
    )(place, table, here, inner, outer, cotangent, weights, *saved)


def back_pass(place, here, inner, outer, packed):
    smem = pl.BlockSpec(memory_space=pltpu.SMEM)
    vmem = pl.BlockSpec(memory_space=pltpu.VMEM)
    return pl.pallas_call(
        back_body,
        out_shape=jax.ShapeDtypeStruct((ROWS * COLS, C), bf16),
        in_specs=[smem] + [vmem] * 4,
        out_specs=vmem,
        scratch_shapes=slot_scratch() + [
            pltpu.VMEM((2, LINE, HALF), f32),
            pltpu.VMEM((EXT, 2, WIN, 8, HALF), f32),
            pltpu.VMEM((EXT, 2, WIN, 8, HALF), f32),
            pltpu.VMEM((2, SLOTS * TAPS, HALF), f32),
            pltpu.VMEM((2, SLOTS * PAIRS, HALF), f32),
            pltpu.VMEM((2, ROWS * COLS, HALF), f32),
        ],
        compiler_params=pltpu.CompilerParams(vmem_limit_bytes=28 * 1024 * 1024),
        cost_estimate=pl.CostEstimate(flops=4_000_000_000, bytes_accessed=8_000_000, transcendentals=0),
        name="back_pass",
    )(place, here, inner, outer, packed)


def core_add_body(keep_ref, other_ref, total_ref):
    total_ref[...] = (keep_ref[...].astype(f32) + other_ref[...].astype(f32)).astype(bf16)


def core_add(keep, other):
    vmem = pl.BlockSpec(memory_space=pltpu.VMEM)
    return pl.pallas_call(
        core_add_body,
        out_shape=jax.ShapeDtypeStruct(keep.shape, bf16),
        in_specs=[vmem] * 2,
        out_specs=vmem,
        compiler_params=pltpu.CompilerParams(vmem_limit_bytes=4 * 1024 * 1024),
        name="core_add",
    )(keep, other)


def swap(block, axis, pairs):
    return lax.ppermute(block, axis, pairs)


LAT_INNER = [(i, i ^ 1) for i in range(8)]
LAT_OUTER = [(i, i + 1 if i % 2 else i - 1) for i in range(1, 7)]
LON_INNER = [(i, i ^ 1) for i in range(32)]
LON_OUTER = [(i, (i + 1 if i % 2 else i - 1) % 32) for i in range(32)]
PLANE = ("y", "x_low", "x_high")


def spread(block, axis):
    return lax.all_to_all(block, axis, 0, 0, tiled=True)


LAT = ("y", "x_low")
LON = ("z", "x_high", "core")
CORE = [(0, 1), (1, 0)]


def beside(block):
    return jnp.stack((block, swap(block, LAT, LAT_INNER), swap(block, LAT, LAT_OUTER)), axis=0)


def around(here):
    return here, swap(here, LON, LON_INNER), swap(here, LON, LON_OUTER)


def z_add(total, bits):
    return total + swap(total, "z", [(i, i ^ bits) for i in range(8)])


def shards(
    field, cotangent, mix_weight, first_weight, first_bias, hidden_weight, hidden_bias,
    output_weight, output_bias, lon_half, lat_half,
):
    flat_cot = cotangent.reshape(-1, C)
    mixed = lax.dot_general(
        flat_cot, mix_weight, (((1,), (1,)), ((), ())), preferred_element_type=f32
    ).astype(bf16)
    parts = around(beside(jnp.stack((field, mixed.reshape(ROWS, COLS, C)), axis=0)))
    lat = lax.axis_index("y") * 2 + lax.axis_index("x_low")
    place = jnp.stack((lat * ROWS, lax.axis_index("core"), lat % 2)).astype(jnp.int32)
    place = jnp.concatenate((place, lon_half, lat_half))
    table = tables(lon_half, lat_half)
    vectors = jnp.concatenate((first_weight, jnp.stack((first_bias, hidden_bias, output_bias))), axis=0)
    weights = jnp.stack((hidden_weight, output_weight))
    kern, ksum, packed, *saved = network_pass(place, table, vectors, weights)
    keep, send = gradient_pass(place, table, *parts, flat_cot, weights, (kern, ksum, *saved))
    total = core_add(keep, swap(send, "core", CORE))
    total, parts = lax.optimization_barrier((total, parts))
    total = spread(total.reshape(16, 8, PACK), PLANE)
    back = back_pass(place, *parts, packed)
    total, back = lax.optimization_barrier((total, back))
    total = jnp.sum(total.astype(f32), axis=0)
    for bits in (1, 2, 6):
        total = z_add(total, bits)
    own = spread(jnp.broadcast_to(total.astype(bf16)[None], (16, 8, PACK)), PLANE).reshape(HALF, PACK)
    mix, hid, out, first, fb, hb, ob = unpack(place, own, swap(own, "core", CORE))
    return (
        back.reshape(ROWS, COLS, C), mix, first, fb.reshape(C), hid, hb.reshape(C), out, ob.reshape(C),
    )


def solution(mesh):
    split = Mesh(mesh.devices.reshape(8, 2, 2, 4, 2), ("z", "x_high", "core", "y", "x_low"))
    grid = P(LAT, LON, None)
    in_specs = (grid, grid) + (P(),) * 9
    out_specs = (grid,) + (P(),) * 7
    return jax.shard_map(shards, mesh=split, in_specs=in_specs, out_specs=out_specs, check_vma=False)
```

time: 94.3 us -> 89 us (0.944)
  blocking collectives: 27.9 us -> 12.6 us
  starting transfers between devices: 23 us -> 29.4 us
  Pallas kernels: 24.3 us -> 29.3 us
  local copies, waits for them, and re-layouts: 5.44 us -> 1.67 us
  other arithmetic: 1.82 us -> 5 us
  waiting for transfers between devices: 10.2 us -> 8.65 us
    all_to_all x2 -> x1, blocking collectives: 27.9 us -> 12.6 us  [spread(): return lax.all_to_all(block, axis, 0, 0, tiled=True)]
    all_to_all x0 -> x1, starting transfers between devices: none -> 6.78 us  [spread(): return lax.all_to_all(block, axis, 0, 0, tiled=True)]
    unnamed x26 -> x4, local copies, waits for them, and re-layouts: 5.42 us -> 0.91 us
    pallas_call x1 -> x3, Pallas kernels: 15.9 us -> 19.9 us  [the longest x1 12.6 us: gradient_pass(): pl.pallas_call(gradient_body, out_shape=(jax.ShapeDtypeStruct((C // 2, PA...]
    ppermute x9, waiting for transfers between devices: 10.2 us -> 7.83 us  [swap(): return lax.ppermute(block, axis, pairs)]
    another operation x4 -> x5, other arithmetic: 1.71 us -> 3.26 us  [the longest x2 1.35 us: tables(): jnp.stack((1.0 / lon, 1.0 / lat, lax.rsqrt((2.0 * lon + 1.0) * (2.0 * lat...]
    pallas_call x1, Pallas kernels: 6.94 us -> 7.88 us  [network_pass(): pl.pallas_call(network_body, out_shape=(jax.ShapeDtypeStruct((2, SLOTS *...]
  transfers between devices with their start and end apart: 9 -> 10, of which waited for: 6 -> 6; matrix products, arithmetic and copies ran while one was open for 1% -> 4% of each run, Pallas kernels for 7% -> 16%
where the time goes in v3:
time: 89 us; the launch traced here: 88.4 us
  starting transfers between devices  29.4 us (33%)
  Pallas kernels  29.3 us (33%)
  blocking collectives  12.6 us (14%)
  waiting for transfers between devices  8.65 us (10%)
  other arithmetic  5 us (6%)
  local copies, waits for them, and re-layouts  1.67 us (2%)
  matrix products  1.03 us (1%)
    ppermute x9, starting transfers between devices, swap(): return lax.ppermute(block, axis, pairs)  22.6 us
    pallas_call x1, Pallas kernels, gradient_pass(): pl.pallas_call(gradient_body, out_shape=(jax.ShapeDtypeStruct((C // 2, PA...  12.6 us
    all_to_all x1, blocking collectives, spread(): return lax.all_to_all(block, axis, 0, 0, tiled=True)  12.6 us
    pallas_call x1, Pallas kernels, network_pass(): pl.pallas_call(network_body, out_shape=(jax.ShapeDtypeStruct((2, SLOTS *...  7.88 us
    ppermute x9, waiting for transfers between devices, swap(): return lax.ppermute(block, axis, pairs)  7.83 us
    all_to_all x1, starting transfers between devices, spread(): return lax.all_to_all(block, axis, 0, 0, tiled=True)  6.78 us
    pallas_call x1, Pallas kernels, back_pass(): pl.pallas_call(back_body, out_shape=jax.ShapeDtypeStruct((ROWS * COLS, C)...  6.56 us
  transfers between devices with their start and end apart: 10, of which 6 were waited for; matrix products, arithmetic and copies ran while one was open for 4% of the time, Pallas kernels for 16%

profile of v3, /device:TPU:1, one launch (start us, length us, event | category | flops | bytes accessed | tf_op | source)
XLA Modules:
  0.0 88.4 jit_solution(16539318665642467699)
XLA Ops:
  0.6 0.9 %copy-done = bf16[256,256]{1,0:T(8,128)(2,1)S(1)} copy-done((bf16[256,256]{1,0:T(8,128)(2,1)S(1)}, bf16[256,256]{1,0:T(8,128)(2,1)}, u32[]{:S(2)}) %copy-start) | copy-done | bytes 131096
  1.5 1.0 %convolution_convert_fusion = bf16[128,256]{1,0:T(8,128)(2,1)S(1)} fusion(bf16[128,256]{1,0:T(8,128)(2,1)} %bitcast.31, bf16[256,256]{1,0:T(8,128)(2,1)S(1)} %copy-done), kind=kOutput, calls=%fused_computation | convolution fusion | flops 16809984 | bytes 262144 | tf_op jit(solution)/shard_map/dot_general | solution.py:617
  2.6 0.9 fusion
  3.4 2.1 %collective-permute-start = (bf16[2,4,32,256]{3,2,1,0:T(8,128)(2,1)S(1)}, bf16[2,4,32,256]{3,2,1,0:T(8,128)(2,1)S(1)}, u32[]{:S(2)}, u32[]{:S(2)}) collective-permute-start(bf16[2,4,32,256]{3,2,1,0:T(8,128)(2,1)S(1)} %get-tuple-element.59), channel_id=1, source_target_pairs={{0,1},{1,0},{2,3},{3,2},{4,5},{5,4},{6,7},{7,6},{8,9},{9,8},{10,11... | collective-permute-start | bytes 393224 | tf_op jit(solution)/shard_map/ppermute | solution.py:581
  6.9 0.7 pad_maximum_fusion.3.vec_ref
  9.1 1.0 %pad_maximum_fusion.1.weight_ref = bf16[2,256,256]{2,1,0:T(8,128)(2,1)S(1)} fusion(bf16[1,256,256]{2,1,0:T(8,128)(2,1)} %bitcast.34, bf16[1,256,256]{2,1,0:T(8,128)(2,1)} %bitcast.35), kind=kLoop, calls=%fused_computation.3 | loop fusion | flops 131072 | bytes 524288 | tf_op jit(solution)/shard_map/stack | solution.py:626
  10.2 3.4 %collective-permute-start.3 = (bf16[3,2,4,32,256]{4,3,2,1,0:T(8,128)(2,1)S(1)}, bf16[3,2,4,32,256]{4,3,2,1,0:T(8,128)(2,1)S(1)}, u32[]{:S(2)}, u32[]{:S(2)}) collective-permute-start(bf16[3,2,4,32,256]{4,3,2,1,0:T(8,128)(2,1)S(1)} %pad_maximum_fusion.here_ref), channel_id=1, source_target_pairs={{0,248},{8,16},{16,8},{24,32},{32,24},{40,48},{48,40},{56,64},{64,... | collective-permute-start | bytes 1179656 | tf_op jit(solution)/shard_map/ppermute | solution.py:581
  13.5 4.8 %collective-permute-start.2 = (bf16[3,2,4,32,256]{4,3,2,1,0:T(8,128)(2,1)S(1)}, bf16[3,2,4,32,256]{4,3,2,1,0:T(8,128)(2,1)S(1)}, u32[]{:S(2)}, u32[]{:S(2)}) collective-permute-start(bf16[3,2,4,32,256]{4,3,2,1,0:T(8,128)(2,1)S(1)} %pad_maximum_fusion.here_ref), channel_id=1, source_target_pairs={{0,8},{8,0},{16,24},{24,16},{32,40},{40,32},{48,56},{56,48},{64,72... | collective-permute-start | bytes 1179656 | tf_op jit(solution)/shard_map/ppermute | solution.py:581
  18.4 7.9 %network_pass.1 = (f32[2,4032,128]{2,1,0:T(8,128)S(1)}, f32[2,2240,128]{2,1,0:T(8,128)S(1)}, bf16[14,288,256]{2,1,0:T(8,128)(2,1)S(1)}, bf16[9,288,256]{2,1,0:T(...) custom-call(s32[67]{0:T(128)S(1)} %concatenate.6.place_ref, ...), custom_call_target="tpu_custom_call" | custom-call | flops 6000000000 | bytes 16000000 | tf_op jit(solution)/shard_map/network_pass/pallas_call | solution.py:212
  26.3 12.6 %gradient_pass.1 = (bf16[128,896]{1,0:T(8,128)(2,1)S(1)}, bf16[128,896]{1,0:T(8,128)(2,1)S(1)}) custom-call(s32[67]{0:T(128)S(1)} %concatenate.6.place_ref, f32[4,32]{1,0:T(4,128)S(1)} %pad_maximum_fusion.4.tab_ref, bf16[3,2,4,32,256]{4,3,2,1,0:T(8,128)(2,1)S(1)} %pad_maximum_fusion.here_ref, ...), custom_call_target="tpu_custom_call" | custom-call | flops 8999999488 | bytes 20000000 | tf_op jit(solution)/shard_map/gradient_pass/pallas_call | solution.py:515
  39.1 1.5 %collective-permute-done.4.other_ref = bf16[128,896]{1,0:T(8,128)(2,1)S(1)} collective-permute-done((bf16[128,896]{1,0:T(8,128)(2,1)S(1)}, bf16[128,896]{1,0:T(8,128)(2,1)S(1)}, u32[]{:S(2)}, u32[]{:S(2)}) %collective-permute-start.4) | collective-permute-done | bytes 229408 | tf_op jit(solution)/shard_map/ppermute | solution.py:581
  41.3 6.8 %all-to-all-start = ((bf16[16,8,896]{2,1,0:T(8,128)(2,1)}), bf16[16,8,896]{2,1,0:T(8,128)(2,1)}, u32[]{:S(2)}, u32[]{:S(2)}) async-start(bf16[16,8,896]{2,1,0:T(8,128)(2,1)} %bitcast.17), calls=%async_computation | async-start | bytes 458752 | tf_op jit(solution)/shard_map/all_to_all | solution.py:592
  48.1 6.6 %back_pass.1 = bf16[128,256]{1,0:T(8,128)(2,1)} custom-call(s32[67]{0:T(128)S(1)} %concatenate.6.place_ref, bf16[3,2,4,32,256]{4,3,2,1,0:T(8,128)(2,1)S(1)} %pad_maximum_fusion.here_ref, bf16[3,2,4,32,256]{4,3,2,1,0:T(8,128)(2,1)S(1)} %collective-permute-done.2.inner_ref, bf16[3,2,4,32,256]{4,3,2,1,0:T(8,128)(2,1)S(1)} %collective-permute-done.3.outer_ref, ...), custom_call_target="tpu_custom_call" | custom-call | flops 4000000000 | bytes 8000000 | tf_op jit(solution)/shard_map/back_pass/pallas_call | solution.py:545
  54.6 0.8 all-to-all-done
  55.5 1.0 %convert_reduce_fusion = f32[8,896]{1,0:T(8,128)S(1)} fusion(bf16[16,8,896]{2,1,0:T(8,128)(2,1)} %all-to-all-done), kind=kLoop, calls=%fused_computation.1 | loop fusion | flops 222208 | bytes 258048 | tf_op jit(solution)/shard_map/reduce_sum | solution.py:634
  56.5 2.7 %collective-permute-done.5 = f32[8,896]{1,0:T(8,128)S(1)} collective-permute-done((f32[8,896]{1,0:T(8,128)S(1)}, f32[8,896]{1,0:T(8,128)S(1)}, u32[]{:S(2)}, u32[]{:S(2)}) %collective-permute-start.5) | collective-permute-done | bytes 28704 | tf_op jit(solution)/shard_map/ppermute | solution.py:581
  59.3 2.4 %collective-permute-start.6 = (f32[8,896]{1,0:T(8,128)S(1)}, f32[8,896]{1,0:T(8,128)S(1)}, u32[]{:S(2)}, u32[]{:S(2)}) collective-permute-start(f32[8,896]{1,0:T(8,128)S(1)} %add.26), channel_id=1, source_target_pairs={{0,64},{32,96},{64,0},{96,32},{128,192},{160,224},{192,128},{224,1... | collective-permute-start | bytes 86024 | tf_op jit(solution)/shard_map/ppermute | solution.py:581
  61.6 1.3 %collective-permute-done.6 = f32[8,896]{1,0:T(8,128)S(1)} collective-permute-done((f32[8,896]{1,0:T(8,128)S(1)}, f32[8,896]{1,0:T(8,128)S(1)}, u32[]{:S(2)}, u32[]{:S(2)}) %collective-permute-start.6) | collective-permute-done | bytes 28704 | tf_op jit(solution)/shard_map/ppermute | solution.py:581
  62.9 3.6 %collective-permute-start.7 = (f32[8,896]{1,0:T(8,128)S(1)}, f32[8,896]{1,0:T(8,128)S(1)}, u32[]{:S(2)}, u32[]{:S(2)}) collective-permute-start(f32[8,896]{1,0:T(8,128)S(1)} %add.27), channel_id=1, source_target_pairs={{0,192},{32,224},{64,128},{96,160},{128,64},{160,96},{192,0},{224,... | collective-permute-start | bytes 86024 | tf_op jit(solution)/shard_map/ppermute | solution.py:581
  66.5 1.3 %collective-permute-done.7 = f32[8,896]{1,0:T(8,128)S(1)} collective-permute-done((f32[8,896]{1,0:T(8,128)S(1)}, f32[8,896]{1,0:T(8,128)S(1)}, u32[]{:S(2)}, u32[]{:S(2)}) %collective-permute-start.7) | collective-permute-done | bytes 28704 | tf_op jit(solution)/shard_map/ppermute | solution.py:581
  67.8 12.6 %all_to_all.10 = bf16[16,8,896]{2,1,0:T(8,128)(2,1)S(1)} all-to-all(bf16[16,8,896]{2,1,0:T(8,128)(2,1)S(1)} %broadcast_in_dim.2), channel_id=1, replica_groups=mesh['z'=8,'x_high'=2,'core'=2,'y'=4,'x_low'=2] {'y','x_low','x_high'}, dimensions={0} | all-to-all | bytes 458752 | tf_op jit(solution)/shard_map/all_to_all | solution.py:592
  80.3 5.5 %collective-permute-start.8 = (bf16[128,896]{1,0:T(8,128)(2,1)S(1)}, bf16[128,896]{1,0:T(8,128)(2,1)S(1)}, u32[]{:S(2)}, u32[]{:S(2)}) collective-permute-start(bf16[128,896]{1,0:T(8,128)(2,1)S(1)} %bitcast.29), channel_id=1, source_target_pairs={{0,8},{8,0},{1,9},{9,1},{2,10},{10,2},{3,11},{11,3},{4,12},{12,4},... | collective-permute-start | bytes 688136 | tf_op jit(solution)/shard_map/ppermute | solution.py:581
  85.9 1.1 %collective-permute-done.8.other_ref = bf16[128,896]{1,0:T(8,128)(2,1)S(1)} collective-permute-done((bf16[128,896]{1,0:T(8,128)(2,1)S(1)}, bf16[128,896]{1,0:T(8,128)(2,1)S(1)}, u32[]{:S(2)}, u32[]{:S(2)}) %collective-permute-start.8) | collective-permute-done | bytes 229408 | tf_op jit(solution)/shard_map/ppermute | solution.py:581
  87.0 1.4 %unpack.1 = (f32[256,256]{1,0:T(8,128)}, f32[256,256]{1,0:T(8,128)}, f32[256,256]{1,0:T(8,128)}, f32[3,256]{1,0:T(4,128)}, f32[1,256]{1,0:T(1,128)}, /*index=5*/f32[1,256]{1,0:T(1,128)}, f32[1,256]{1,0:T(1,128)}) custom-call(s32[67]{0:T(128)S(1)} %concatenate.6.place_ref, bf16[128,896]{1,0:T(8,128)(2,1)S(1)} %bitcast.30, ...), custom_call_target="tpu_custom_call" | custom-call | tf_op jit(solution)/shard_map/unpack/pallas_call | solution.py:491
  (19 shorter events, 3.8 us)
Async XLA Ops:
  0.6 0.9 %copy-start = (bf16[256,256]{1,0:T(8,128)(2,1)S(1)}, bf16[256,256]{1,0:T(8,128)(2,1)}, u32[]{:S(2)}) copy-start(bf16[256,256]{1,0:T(8,128)(2,1)} %param.14) | copy-start | bytes 393220
  3.4 6.6 %collective-permute-start = (bf16[2,4,32,256]{3,2,1,0:T(8,128)(2,1)S(1)}, bf16[2,4,32,256]{3,2,1,0:T(8,128)(2,1)S(1)}, u32[]{:S(2)}, u32[]{:S(2)}) collective-permute-start(bf16[2,4,32,256]{3,2,1,0:T(8,128)(2,1)S(1)} %get-tuple-element.59), channel_id=1, source_target_pairs={{0,1},{1,0},{2,3},{3,2},{4,5},{5,4},{6,7},{7,6},{8,9},{9,8},{10,11... | collective-permute-start | bytes 393224 | tf_op jit(solution)/shard_map/ppermute | solution.py:581
  5.6 4.5 %collective-permute-start.1 = (bf16[2,4,32,256]{3,2,1,0:T(8,128)(2,1)S(1)}, bf16[2,4,32,256]{3,2,1,0:T(8,128)(2,1)S(1)}, u32[]{:S(2)}, u32[]{:S(2)}) collective-permute-start(bf16[2,4,32,256]{3,2,1,0:T(8,128)(2,1)S(1)} %get-tuple-element.59), channel_id=1, source_target_pairs={{1,2},{2,1},{3,4},{4,3},{5,6},{6,5},{9,10},{10,9},{11,12},{12,11},... | collective-permute-start | bytes 393224 | tf_op jit(solution)/shard_map/ppermute | solution.py:581
  10.2 16.1 %copy-start.1 = (bf16[4,32,256]{2,1,0:T(8,128)(2,1)S(1)}, bf16[4,32,256]{2,1,0:T(8,128)(2,1)}, u32[]{:S(2)}) copy-start(bf16[4,32,256]{2,1,0:T(8,128)(2,1)} %param.13) | copy-start | bytes 196612
  10.2 16.1 %collective-permute-start.3 = (bf16[3,2,4,32,256]{4,3,2,1,0:T(8,128)(2,1)S(1)}, bf16[3,2,4,32,256]{4,3,2,1,0:T(8,128)(2,1)S(1)}, u32[]{:S(2)}, u32[]{:S(2)}) collective-permute-start(bf16[3,2,4,32,256]{4,3,2,1,0:T(8,128)(2,1)S(1)} %pad_maximum_fusion.here_ref), channel_id=1, source_target_pairs={{0,248},{8,16},{16,8},{24,32},{32,24},{40,48},{48,40},{56,64},{64,... | collective-permute-start | bytes 1179656 | tf_op jit(solution)/shard_map/ppermute | solution.py:581
  13.5 12.7 %collective-permute-start.2 = (bf16[3,2,4,32,256]{4,3,2,1,0:T(8,128)(2,1)S(1)}, bf16[3,2,4,32,256]{4,3,2,1,0:T(8,128)(2,1)S(1)}, u32[]{:S(2)}, u32[]{:S(2)}) collective-permute-start(bf16[3,2,4,32,256]{4,3,2,1,0:T(8,128)(2,1)S(1)} %pad_maximum_fusion.here_ref), channel_id=1, source_target_pairs={{0,8},{8,0},{16,24},{24,16},{32,40},{40,32},{48,56},{56,48},{64,72... | collective-permute-start | bytes 1179656 | tf_op jit(solution)/shard_map/ppermute | solution.py:581
  39.0 1.6 %collective-permute-start.4 = (bf16[128,896]{1,0:T(8,128)(2,1)S(1)}, bf16[128,896]{1,0:T(8,128)(2,1)S(1)}, u32[]{:S(2)}, u32[]{:S(2)}) collective-permute-start(bf16[128,896]{1,0:T(8,128)(2,1)S(1)} %get-tuple-element.43), channel_id=1, source_target_pairs={{0,8},{8,0},{1,9},{9,1},{2,10},{10,2},{3,11},{11,3},{4,12},{12,4},... | collective-permute-start | bytes 688136 | tf_op jit(solution)/shard_map/ppermute | solution.py:581
  41.3 14.2 %all-to-all-start = ((bf16[16,8,896]{2,1,0:T(8,128)(2,1)}), bf16[16,8,896]{2,1,0:T(8,128)(2,1)}, u32[]{:S(2)}, u32[]{:S(2)}) async-start(bf16[16,8,896]{2,1,0:T(8,128)(2,1)} %bitcast.17), calls=%async_computation | async-start | bytes 458752 | tf_op jit(solution)/shard_map/all_to_all | solution.py:592
  56.4 2.8 %collective-permute-start.5 = (f32[8,896]{1,0:T(8,128)S(1)}, f32[8,896]{1,0:T(8,128)S(1)}, u32[]{:S(2)}, u32[]{:S(2)}) collective-permute-start(f32[8,896]{1,0:T(8,128)S(1)} %convert_reduce_fusion), channel_id=1, source_target_pairs={{0,32},{32,0},{64,96},{96,64},{128,160},{160,128},{192,224},{224,1... | collective-permute-start | bytes 86024 | tf_op jit(solution)/shard_map/ppermute | solution.py:581
  59.3 3.6 %collective-permute-start.6 = (f32[8,896]{1,0:T(8,128)S(1)}, f32[8,896]{1,0:T(8,128)S(1)}, u32[]{:S(2)}, u32[]{:S(2)}) collective-permute-start(f32[8,896]{1,0:T(8,128)S(1)} %add.26), channel_id=1, source_target_pairs={{0,64},{32,96},{64,0},{96,32},{128,192},{160,224},{192,128},{224,1... | collective-permute-start | bytes 86024 | tf_op jit(solution)/shard_map/ppermute | solution.py:581
  62.9 4.8 %collective-permute-start.7 = (f32[8,896]{1,0:T(8,128)S(1)}, f32[8,896]{1,0:T(8,128)S(1)}, u32[]{:S(2)}, u32[]{:S(2)}) collective-permute-start(f32[8,896]{1,0:T(8,128)S(1)} %add.27), channel_id=1, source_target_pairs={{0,192},{32,224},{64,128},{96,160},{128,64},{160,96},{192,0},{224,... | collective-permute-start | bytes 86024 | tf_op jit(solution)/shard_map/ppermute | solution.py:581
  80.3 6.6 %collective-permute-start.8 = (bf16[128,896]{1,0:T(8,128)(2,1)S(1)}, bf16[128,896]{1,0:T(8,128)(2,1)S(1)}, u32[]{:S(2)}, u32[]{:S(2)}) collective-permute-start(bf16[128,896]{1,0:T(8,128)(2,1)S(1)} %bitcast.29), channel_id=1, source_target_pairs={{0,8},{8,0},{1,9},{9,1},{2,10},{10,2},{3,11},{11,3},{4,12},{12,4},... | collective-permute-start | bytes 688136 | tf_op jit(solution)/shard_map/ppermute | solution.py:581

commit v4 on v3

--- a/solution.py
+++ b/solution.py
@@ -127,11 +127,11 @@
 def lay_taps(g, taps, kern, ksum):
     wide = taps.astype(f32)
     at = pl.multiple_of(g * SPAN, 8)
-    kern[0, pl.ds(at, SPAN), :] = wide[:, :HALF]
-    kern[1, pl.ds(at, SPAN), :] = wide[:, HALF:]
+    for h in range(kern.shape[0]):
+        kern[h, pl.ds(at, SPAN), :] = wide[:, h * HALF:(h + 1) * HALF]
     for q in range(GROUP):
         to = pl.multiple_of((GROUP * g + q) * PAIRS, 8)
-        for h in range(2):
+        for h in range(kern.shape[0]):
             even = kern[h, pl.ds(at + q * TAPS, PAIRS - 4, stride=2), :]
             odd = kern[h, pl.ds(at + q * TAPS + 1, PAIRS - 4, stride=2), :]
             ksum[h, pl.ds(to, PAIRS - 4), :] = even + odd
@@ -242,7 +242,7 @@
     )(place, table, vectors, weights)
 
 
-def build_windows(place_ref, here_ref, inner_ref, outer_ref, which, front, line, window, change):
+def build_windows(place_ref, read_here, read_inner, read_outer, halves, front, line, window, change):
     lat_odd = place_ref[2] == 1
     left_inner = place_ref[1] == 1
 
@@ -252,16 +252,16 @@
             band = e // ROWS
             part = jnp.where(band == 1, 0, jnp.where((band == 2) == lat_odd, 2, 1))
             row = e % ROWS
-            for n in range(2):
-                lanes = slice(n * HALF, (n + 1) * HALF)
-                near = inner_ref[part, which, row, :, lanes].astype(f32)
-                far = outer_ref[part, which, row, :, lanes].astype(f32)
+            for n, h in enumerate(halves):
+                lanes = slice(h * HALF, (h + 1) * HALF)
+                near = read_inner(part, row, lanes).astype(f32)
+                far = read_outer(part, row, lanes).astype(f32)
                 line[n, 0:8] = jnp.zeros((8, HALF), f32)
                 line[n, 96:LINE] = jnp.zeros((LINE - 96, HALF), f32)
                 line[n, front:front + 32] = jnp.where(left_inner, near, far)
-                line[n, front + 32:front + 64] = here_ref[part, which, row, :, lanes].astype(f32)
+                line[n, front + 32:front + 64] = read_here(part, row, lanes).astype(f32)
                 line[n, front + 64:front + 96] = jnp.where(left_inner, far, near)
-            for n in range(2):
+            for n in range(len(halves)):
                 last = None
                 for p in range(WIN):
                     value = line[n, pl.ds(p, 8, stride=4), :]
@@ -294,7 +294,7 @@
 def gradient_body(
     place_ref, tab_ref, here_ref, inner_ref, outer_ref, cot_ref, weight_ref,
     kern, ksum, h1_ref, h2_ref, c2_ref, sin_lon, cos_lon, sin_lat, cos_lat,
-    keep_ref, send_ref,
+    keep_ref, send_ref, cots_ref,
     slot_row, slot_tap, first_slot, low_tap, high_tap,
     line, window, change, mine_line, grad, conv, d_mix, d_out, d_hid, d_small, d_side,
 ):
@@ -304,7 +304,14 @@
     core = place_ref[1]
     for h in range(2):
         mine_line[h] = here_ref[0, 1, :, :, h * HALF:(h + 1) * HALF].reshape(ROWS * COLS, HALF).astype(f32)
-    build_windows(place_ref, here_ref, inner_ref, outer_ref, 0, 0, line, window, change)
+    def reader(ref):
+        return lambda part, row, lanes: ref[part, 0, row, :, lanes]
+
+    for n, ref in enumerate((here_ref, inner_ref, outer_ref)):
+        cots_ref[n] = ref[:, 1]
+    build_windows(
+        place_ref, reader(here_ref), reader(inner_ref), reader(outer_ref), (0, 1), 0, line, window, change
+    )
     sub = lax.broadcasted_iota(jnp.int32, (8, HALF), 0)
     masks = [(sub & bit) == 0 for bit in (1, 2, 4)]
     zero = jnp.zeros((8, HALF), f32)
@@ -415,18 +422,20 @@
             target[:, q * C:q * C + part.shape[1]] = part.astype(bf16)
 
 
-def back_body(
-    place_ref, here_ref, inner_ref, outer_ref, packed, gfield_ref,
-    slot_row, slot_tap, first_slot, low_tap, high_tap, line, window, change, kern, ksum, back,
-):
+def back_body(half, place_ref, cots_ref, packed, *rest):
+    first_ref = rest[0] if half else None
+    gfield_ref, slot_row, slot_tap, first_slot, low_tap, high_tap, line, window, change, kern, ksum, back = rest[half:]
     _, slot_count = number_slots(place_ref, slot_row, slot_tap, first_slot, low_tap, high_tap)
 
     def lay(g, _):
-        lay_taps(g, packed[g], kern, ksum)
+        lay_taps(g, packed[g, :, half * HALF:(half + 1) * HALF], kern, ksum)
         return 0
 
     lax.fori_loop(0, (slot_count + GROUP - 1) // GROUP, lay, 0)
-    build_windows(place_ref, here_ref, inner_ref, outer_ref, 1, 8, line, window, change)
+    def reader(n):
+        return lambda part, row, lanes: cots_ref[n, part, row, :, lanes]
+
+    build_windows(place_ref, reader(0), reader(1), reader(2), (half,), 8, line, window, change)
     zero = jnp.zeros((8, HALF), f32)
 
     def back_row(r, _):
@@ -442,32 +451,31 @@
                 start = HLON + 1 + w - 8 * b
                 at = slot * TAPS + 8 * b
                 pair = slot * PAIRS + 4 * b
-                new = []
-                for h in range(2):
-                    acc = list(total[6 * h:6 * h + 6])
-                    odd, fall, next_fall = taps_of(window, change, e, h, start)
-                    for j in range(4):
-                        k_sum = row_of(ksum, h, pair + 3 - j)
-                        k_even = row_of(kern, h, at + 7 - 2 * j)
-                        k_odd = row_of(kern, h, at + 6 - 2 * j)
-                        for m in range(2):
-                            acc[m] = acc[m] + k_sum * odd[m + j]
-                            acc[2 + m] = acc[2 + m] + k_even * fall[m + j]
-                            acc[4 + m] = acc[4 + m] + k_odd * next_fall[m + j]
-                    new += acc
-                return tuple(new)
+                acc = list(total)
+                odd, fall, next_fall = taps_of(window, change, e, 0, start)
+                for j in range(4):
+                    k_sum = row_of(ksum, 0, pair + 3 - j)
+                    k_even = row_of(kern, 0, at + 7 - 2 * j)
+                    k_odd = row_of(kern, 0, at + 6 - 2 * j)
+                    for m in range(2):
+                        acc[m] = acc[m] + k_sum * odd[m + j]
+                        acc[2 + m] = acc[2 + m] + k_even * fall[m + j]
+                        acc[4 + m] = acc[4 + m] + k_odd * next_fall[m + j]
+                return tuple(acc)
 
             return lax.fori_loop(0, blocks, one_block, total)
 
-        total = lax.fori_loop(r, r + TLAT, one_source, (zero,) * 12)
-        for h in range(2):
-            for t, value in enumerate(combine(total[6 * h:6 * h + 6])):
-                back[h, pl.ds(r * COLS + t, 8, stride=4), :] = value
+        total = lax.fori_loop(r, r + TLAT, one_source, (zero,) * 6)
+        for t, value in enumerate(combine(total)):
+            back[pl.ds(r * COLS + t, 8, stride=4), :] = value
         return 0
 
     lax.fori_loop(0, ROWS, back_row, 0)
-    for h in range(2):
-        gfield_ref[:, h * HALF:(h + 1) * HALF] = back[h].astype(bf16)
+    if half:
+        gfield_ref[:, :HALF] = first_ref[...]
+        gfield_ref[:, HALF:] = back[...].astype(bf16)
+    else:
+        gfield_ref[...] = back[...].astype(bf16)
 
 
 def unpack_body(place_ref, own_ref, other_ref, mix_ref, hid_ref, out_ref, first_ref, fb_ref, hb_ref, ob_ref, side):
@@ -517,9 +525,10 @@
         out_shape=(
             jax.ShapeDtypeStruct((C // 2, PACK), bf16),
             jax.ShapeDtypeStruct((C // 2, PACK), bf16),
+            jax.ShapeDtypeStruct((3, 3, ROWS, COLS, C), bf16),
         ),
         in_specs=[smem] * 2 + [vmem] * 14,
-        out_specs=(vmem,) * 2,
+        out_specs=(vmem,) * 3,
         scratch_shapes=slot_scratch() + [
             pltpu.VMEM((2, LINE, HALF), f32),
             pltpu.VMEM((EXT, 2, WIN, 8, HALF), f32),
@@ -539,26 +548,26 @@
     )(place, table, here, inner, outer, cotangent, weights, *saved)
 
 
-def back_pass(place, here, inner, outer, packed):
+def back_pass(half, place, cots, packed, *first):
     smem = pl.BlockSpec(memory_space=pltpu.SMEM)
     vmem = pl.BlockSpec(memory_space=pltpu.VMEM)
     return pl.pallas_call(
-        back_body,
-        out_shape=jax.ShapeDtypeStruct((ROWS * COLS, C), bf16),
-        in_specs=[smem] + [vmem] * 4,
+        functools.partial(back_body, half),
+        out_shape=jax.ShapeDtypeStruct((ROWS * COLS, C if half else HALF), bf16),
+        in_specs=[smem] + [vmem] * (2 + half),
         out_specs=vmem,
         scratch_shapes=slot_scratch() + [
-            pltpu.VMEM((2, LINE, HALF), f32),
-            pltpu.VMEM((EXT, 2, WIN, 8, HALF), f32),
-            pltpu.VMEM((EXT, 2, WIN, 8, HALF), f32),
-            pltpu.VMEM((2, SLOTS * TAPS, HALF), f32),
-            pltpu.VMEM((2, SLOTS * PAIRS, HALF), f32),
-            pltpu.VMEM((2, ROWS * COLS, HALF), f32),
+            pltpu.VMEM((1, LINE, HALF), f32),
+            pltpu.VMEM((EXT, 1, WIN, 8, HALF), f32),
+            pltpu.VMEM((EXT, 1, WIN, 8, HALF), f32),
+            pltpu.VMEM((1, SLOTS * TAPS, HALF), f32),
+            pltpu.VMEM((1, SLOTS * PAIRS, HALF), f32),
+            pltpu.VMEM((ROWS * COLS, HALF), f32),
         ],
-        compiler_params=pltpu.CompilerParams(vmem_limit_bytes=28 * 1024 * 1024),
-        cost_estimate=pl.CostEstimate(flops=4_000_000_000, bytes_accessed=8_000_000, transcendentals=0),
-        name="back_pass",
-    )(place, here, inner, outer, packed)
+        compiler_params=pltpu.CompilerParams(vmem_limit_bytes=16 * 1024 * 1024),
+        cost_estimate=pl.CostEstimate(flops=2_500_000_000, bytes_accessed=4_000_000, transcendentals=0),
+        name=f"back_pass_{half}",
+    )(place, cots, packed, *first)
 
 
 def core_add_body(keep_ref, other_ref, total_ref):
@@ -625,16 +634,19 @@
     vectors = jnp.concatenate((first_weight, jnp.stack((first_bias, hidden_bias, output_bias))), axis=0)
     weights = jnp.stack((hidden_weight, output_weight))
     kern, ksum, packed, *saved = network_pass(place, table, vectors, weights)
-    keep, send = gradient_pass(place, table, *parts, flat_cot, weights, (kern, ksum, *saved))
+    keep, send, cots = gradient_pass(place, table, *parts, flat_cot, weights, (kern, ksum, *saved))
     total = core_add(keep, swap(send, "core", CORE))
-    total, parts = lax.optimization_barrier((total, parts))
+    total, cots = lax.optimization_barrier((total, cots))
     total = spread(total.reshape(16, 8, PACK), PLANE)
-    back = back_pass(place, *parts, packed)
+    back = back_pass(0, place, cots, packed)
     total, back = lax.optimization_barrier((total, back))
     total = jnp.sum(total.astype(f32), axis=0)
     for bits in (1, 2, 6):
         total = z_add(total, bits)
-    own = spread(jnp.broadcast_to(total.astype(bf16)[None], (16, 8, PACK)), PLANE).reshape(HALF, PACK)
+    total, cots = lax.optimization_barrier((total.astype(bf16), cots))
+    own = spread(jnp.broadcast_to(total[None], (16, 8, PACK)), PLANE).reshape(HALF, PACK)
+    back = back_pass(1, place, cots, packed, back)
+    own, back = lax.optimization_barrier((own, back))
     mix, hid, out, first, fb, hb, ob = unpack(place, own, swap(own, "core", CORE))
     return (
         back.reshape(ROWS, COLS, C), mix, first, fb.reshape(C), hid, hb.reshape(C), out, ob.reshape(C),

time: 89 us -> 88.1 us (0.990)
  blocking collectives: 12.6 us -> 0 us
  starting transfers between devices: 29.4 us -> 36.2 us
  waiting for transfers between devices: 8.65 us -> 13.7 us
  other arithmetic: 5 us -> 4.06 us
    all_to_all x1 -> x0, blocking collectives: 12.6 us -> none  [spread(): return lax.all_to_all(block, axis, 0, 0, tiled=True)]
    all_to_all x1 -> x2, starting transfers between devices: 6.78 us -> 13.2 us  [spread(): return lax.all_to_all(block, axis, 0, 0, tiled=True)]
    all_to_all x1 -> x2, waiting for transfers between devices: 0.82 us -> 5.43 us  [spread(): return lax.all_to_all(block, axis, 0, 0, tiled=True)]
    pallas_call x1 -> x2, Pallas kernels: 6.56 us -> 9.08 us  [back_pass(): pl.pallas_call(functools.partial(back_body, half), out_shape=jax.ShapeDty...]
    pallas_call x1, Pallas kernels: 7.88 us -> 6.43 us  [network_pass(): pl.pallas_call(network_body, out_shape=(jax.ShapeDtypeStruct((2, SLOTS *...]
    pallas_call x1, Pallas kernels: 12.6 us -> 11.4 us  [gradient_pass(): pl.pallas_call(gradient_body, out_shape=(jax.ShapeDtypeStruct((C // 2, PA...]
    reduce_sum x1, other arithmetic: 0.98 us -> 0.04 us  [shards(): total = jnp.sum(total.astype(f32), axis=0)]
  transfers between devices with their start and end apart: 10 -> 11, of which waited for: 6 -> 7; matrix products, arithmetic and copies ran while one was open for 4% -> 4% of each run, Pallas kernels for 16% -> 18%
where the time goes in v4:
time: 88.1 us; the launch traced here: 87.3 us
  starting transfers between devices  36.2 us (41%)
  Pallas kernels  29.1 us (33%)
  waiting for transfers between devices  13.7 us (16%)
  other arithmetic  4.06 us (5%)
  local copies, waits for them, and re-layouts  2.36 us (3%)
  matrix products  1.03 us (1%)
    ppermute x9, starting transfers between devices, swap(): return lax.ppermute(block, axis, pairs)  23 us
    all_to_all x2, starting transfers between devices, spread(): return lax.all_to_all(block, axis, 0, 0, tiled=True)  13.2 us
    pallas_call x1, Pallas kernels, gradient_pass(): pl.pallas_call(gradient_body, out_shape=(jax.ShapeDtypeStruct((C // 2, PA...  11.4 us
    pallas_call x2, Pallas kernels, back_pass(): pl.pallas_call(functools.partial(back_body, half), out_shape=jax.ShapeDty...  9.08 us
    ppermute x9, waiting for transfers between devices, swap(): return lax.ppermute(block, axis, pairs)  8.31 us
    pallas_call x1, Pallas kernels, network_pass(): pl.pallas_call(network_body, out_shape=(jax.ShapeDtypeStruct((2, SLOTS *...  6.43 us
    all_to_all x2, waiting for transfers between devices, spread(): return lax.all_to_all(block, axis, 0, 0, tiled=True)  5.43 us
  transfers between devices with their start and end apart: 11, of which 7 were waited for; matrix products, arithmetic and copies ran while one was open for 4% of the time, Pallas kernels for 18%

profile of v4, /device:TPU:1, one launch (start us, length us, event | category | flops | bytes accessed | tf_op | source)
XLA Modules:
  0.0 87.3 jit_solution(14775929768151359752)
XLA Ops:
  0.6 0.9 %copy-done = bf16[256,256]{1,0:T(8,128)(2,1)S(1)} copy-done((bf16[256,256]{1,0:T(8,128)(2,1)S(1)}, bf16[256,256]{1,0:T(8,128)(2,1)}, u32[]{:S(2)}) %copy-start) | copy-done | bytes 131096
  1.5 1.0 %convolution_convert_fusion = bf16[128,256]{1,0:T(8,128)(2,1)S(1)} fusion(bf16[128,256]{1,0:T(8,128)(2,1)} %bitcast.31, bf16[256,256]{1,0:T(8,128)(2,1)S(1)} %copy-done), kind=kOutput, calls=%fused_computation | convolution fusion | flops 16809984 | bytes 262144 | tf_op jit(solution)/shard_map/dot_general | solution.py:626
  2.6 0.9 fusion
  3.4 2.1 %collective-permute-start = (bf16[2,4,32,256]{3,2,1,0:T(8,128)(2,1)S(1)}, bf16[2,4,32,256]{3,2,1,0:T(8,128)(2,1)S(1)}, u32[]{:S(2)}, u32[]{:S(2)}) collective-permute-start(bf16[2,4,32,256]{3,2,1,0:T(8,128)(2,1)S(1)} %get-tuple-element.65), channel_id=1, source_target_pairs={{0,1},{1,0},{2,3},{3,2},{4,5},{5,4},{6,7},{7,6},{8,9},{9,8},{10,11... | collective-permute-start | bytes 393224 | tf_op jit(solution)/shard_map/ppermute | solution.py:590
  9.1 1.0 %pad_maximum_fusion.1.weight_ref = bf16[2,256,256]{2,1,0:T(8,128)(2,1)S(1)} fusion(bf16[1,256,256]{2,1,0:T(8,128)(2,1)} %bitcast.34, bf16[1,256,256]{2,1,0:T(8,128)(2,1)} %bitcast.35), kind=kLoop, calls=%fused_computation.3 | loop fusion | flops 131072 | bytes 524288 | tf_op jit(solution)/shard_map/stack | solution.py:635
  10.2 3.4 %collective-permute-start.3 = (bf16[3,2,4,32,256]{4,3,2,1,0:T(8,128)(2,1)S(1)}, bf16[3,2,4,32,256]{4,3,2,1,0:T(8,128)(2,1)S(1)}, u32[]{:S(2)}, u32[]{:S(2)}) collective-permute-start(bf16[3,2,4,32,256]{4,3,2,1,0:T(8,128)(2,1)S(1)} %pad_maximum_fusion.here_ref), channel_id=1, source_target_pairs={{0,248},{8,16},{16,8},{24,32},{32,24},{40,48},{48,40},{56,64},{64,... | collective-permute-start | bytes 1179656 | tf_op jit(solution)/shard_map/ppermute | solution.py:590
  13.5 4.8 %collective-permute-start.2 = (bf16[3,2,4,32,256]{4,3,2,1,0:T(8,128)(2,1)S(1)}, bf16[3,2,4,32,256]{4,3,2,1,0:T(8,128)(2,1)S(1)}, u32[]{:S(2)}, u32[]{:S(2)}) collective-permute-start(bf16[3,2,4,32,256]{4,3,2,1,0:T(8,128)(2,1)S(1)} %pad_maximum_fusion.here_ref), channel_id=1, source_target_pairs={{0,8},{8,0},{16,24},{24,16},{32,40},{40,32},{48,56},{56,48},{64,72... | collective-permute-start | bytes 1179656 | tf_op jit(solution)/shard_map/ppermute | solution.py:590
  18.4 6.4 %network_pass.1 = (f32[2,4032,128]{2,1,0:T(8,128)S(1)}, f32[2,2240,128]{2,1,0:T(8,128)S(1)}, bf16[14,288,256]{2,1,0:T(8,128)(2,1)S(1)}, bf16[9,288,256]{2,1,0:T(...) custom-call(s32[67]{0:T(128)S(1)} %concatenate.6.place_ref, ...), custom_call_target="tpu_custom_call" | custom-call | flops 6000000000 | bytes 16000000 | tf_op jit(solution)/shard_map/network_pass/pallas_call | solution.py:212
  24.9 11.4 %gradient_pass.1 = (bf16[128,896]{1,0:T(8,128)(2,1)S(1)}, bf16[128,896]{1,0:T(8,128)(2,1)S(1)}, bf16[3,3,4,32,256]{4,3,2,1,0:T(8,128)(2,1)S(1)}) custom-call(s32[67]{0:T(128)S(1)} %concatenate.6.place_ref, f32[4,32]{1,0:T(4,128)S(1)} %pad_maximum_fusion.4.tab_ref, bf16[3,2,4,32,256]{4,3,2,1,0:T(8,128)(2,1)S(1)} %pad_maximum_fusion.here_ref, ...), custom_call_target="tpu_custom_call" | custom-call | flops 8999999488 | bytes 20000000 | tf_op jit(solution)/shard_map/gradient_pass/pallas_call | solution.py:523
  36.3 1.5 %collective-permute-done.4.other_ref = bf16[128,896]{1,0:T(8,128)(2,1)S(1)} collective-permute-done((bf16[128,896]{1,0:T(8,128)(2,1)S(1)}, bf16[128,896]{1,0:T(8,128)(2,1)S(1)}, u32[]{:S(2)}, u32[]{:S(2)}) %collective-permute-start.4) | collective-permute-done | bytes 229408 | tf_op jit(solution)/shard_map/ppermute | solution.py:590
  38.6 9.6 %all-to-all-start = ((bf16[16,8,896]{2,1,0:T(8,128)(2,1)}), bf16[16,8,896]{2,1,0:T(8,128)(2,1)S(1)}, u32[]{:S(2)}, u32[]{:S(2)}) async-start(bf16[16,8,896]{2,1,0:T(8,128)(2,1)} %bitcast.17), calls=%async_computation | async-start | bytes 458752 | tf_op jit(solution)/shard_map/all_to_all | solution.py:601
  48.2 4.2 %back_pass_0.1.rest_0_ = bf16[128,128]{1,0:T(8,128)(2,1)S(1)} custom-call(s32[67]{0:T(128)S(1)} %concatenate.6.place_ref, bf16[3,3,4,32,256]{4,3,2,1,0:T(8,128)(2,1)S(1)} %get-tuple-element.53.cots_ref, bf16[14,288,256]{2,1,0:T(8,128)(2,1)S(1)} %get-tuple-element.50.packed), custom_call_target="tpu_custom_call" | custom-call | flops 2500000000 | bytes 4000000 | tf_op jit(solution)/shard_map/back_pass_0/pallas_call | solution.py:554
  52.4 3.1 %all-to-all-done = bf16[16,8,896]{2,1,0:T(8,128)(2,1)S(1)} async-done(((bf16[16,8,896]{2,1,0:T(8,128)(2,1)}), bf16[16,8,896]{2,1,0:T(8,128)(2,1)S(1)}, u32[]{:S(2)}, u32[]{:S(2)}) %all-to-all-start) | async-done | bytes 229408 | tf_op jit(solution)/shard_map/all_to_all | solution.py:601
  55.7 2.7 %collective-permute-done.5 = f32[8,896]{1,0:T(8,128)S(1)} collective-permute-done((f32[8,896]{1,0:T(8,128)S(1)}, f32[8,896]{1,0:T(8,128)S(1)}, u32[]{:S(2)}, u32[]{:S(2)}) %collective-permute-start.5) | collective-permute-done | bytes 28704 | tf_op jit(solution)/shard_map/ppermute | solution.py:590
  58.4 1.9 %collective-permute-start.6 = (f32[8,896]{1,0:T(8,128)S(1)}, f32[8,896]{1,0:T(8,128)S(1)}, u32[]{:S(2)}, u32[]{:S(2)}) collective-permute-start(f32[8,896]{1,0:T(8,128)S(1)} %add.26), channel_id=1, source_target_pairs={{0,64},{32,96},{64,0},{96,32},{128,192},{160,224},{192,128},{224,1... | collective-permute-start | bytes 86024 | tf_op jit(solution)/shard_map/ppermute | solution.py:590
  60.3 1.7 %collective-permute-done.6 = f32[8,896]{1,0:T(8,128)S(1)} collective-permute-done((f32[8,896]{1,0:T(8,128)S(1)}, f32[8,896]{1,0:T(8,128)S(1)}, u32[]{:S(2)}, u32[]{:S(2)}) %collective-permute-start.6) | collective-permute-done | bytes 28704 | tf_op jit(solution)/shard_map/ppermute | solution.py:590
  62.0 3.6 %collective-permute-start.7 = (f32[8,896]{1,0:T(8,128)S(1)}, f32[8,896]{1,0:T(8,128)S(1)}, u32[]{:S(2)}, u32[]{:S(2)}) collective-permute-start(f32[8,896]{1,0:T(8,128)S(1)} %add.27), channel_id=1, source_target_pairs={{0,192},{32,224},{64,128},{96,160},{128,64},{160,96},{192,0},{224,... | collective-permute-start | bytes 86024 | tf_op jit(solution)/shard_map/ppermute | solution.py:590
  65.6 1.3 %collective-permute-done.7 = f32[8,896]{1,0:T(8,128)S(1)} collective-permute-done((f32[8,896]{1,0:T(8,128)S(1)}, f32[8,896]{1,0:T(8,128)S(1)}, u32[]{:S(2)}, u32[]{:S(2)}) %collective-permute-start.7) | collective-permute-done | bytes 28704 | tf_op jit(solution)/shard_map/ppermute | solution.py:590
  67.6 3.5 %all-to-all-start.1 = ((bf16[16,8,896]{2,1,0:T(8,128)(2,1)}), bf16[16,8,896]{2,1,0:T(8,128)(2,1)S(1)}, u32[]{:S(2)}, u32[]{:S(2)}) async-start(bf16[16,8,896]{2,1,0:T(8,128)(2,1)} %broadcast_in_dim.2), calls=%async_computation.1 | async-start | bytes 458752 | tf_op jit(solution)/shard_map/all_to_all | solution.py:601
  71.1 4.9 %back_pass_1.1 = bf16[128,256]{1,0:T(8,128)(2,1)} custom-call(s32[67]{0:T(128)S(1)} %concatenate.6.place_ref, bf16[3,3,4,32,256]{4,3,2,1,0:T(8,128)(2,1)S(1)} %get-tuple-element.53.cots_ref, bf16[14,288,256]{2,1,0:T(8,128)(2,1)S(1)} %get-tuple-element.50.packed, bf16[128,128]{1,0:T(8,128)(2,1)S(1)} %back_pass_0.1.rest_0_), custom_call_target="tpu_custom_call" | custom-call | flops 2500000000 | bytes 4000000 | tf_op jit(solution)/shard_map/back_pass_1/pallas_call | solution.py:554
  76.0 2.3 %all-to-all-done.1 = bf16[16,8,896]{2,1,0:T(8,128)(2,1)S(1)} async-done(((bf16[16,8,896]{2,1,0:T(8,128)(2,1)}), bf16[16,8,896]{2,1,0:T(8,128)(2,1)S(1)}, u32[]{:S(2)}, u32[]{:S(2)}) %all-to-all-start.1) | async-done | bytes 229408 | tf_op jit(solution)/shard_map/all_to_all | solution.py:601
  78.3 6.4 %collective-permute-start.8 = (bf16[128,896]{1,0:T(8,128)(2,1)S(1)}, bf16[128,896]{1,0:T(8,128)(2,1)S(1)}, u32[]{:S(2)}, u32[]{:S(2)}) collective-permute-start(bf16[128,896]{1,0:T(8,128)(2,1)S(1)} %bitcast.29), channel_id=1, source_target_pairs={{0,8},{8,0},{1,9},{9,1},{2,10},{10,2},{3,11},{11,3},{4,12},{12,4},... | collective-permute-start | bytes 688136 | tf_op jit(solution)/shard_map/ppermute | solution.py:590
  84.7 1.1 %collective-permute-done.8.other_ref = bf16[128,896]{1,0:T(8,128)(2,1)S(1)} collective-permute-done((bf16[128,896]{1,0:T(8,128)(2,1)S(1)}, bf16[128,896]{1,0:T(8,128)(2,1)S(1)}, u32[]{:S(2)}, u32[]{:S(2)}) %collective-permute-start.8) | collective-permute-done | bytes 229408 | tf_op jit(solution)/shard_map/ppermute | solution.py:590
  85.8 1.4 %unpack.1 = (f32[256,256]{1,0:T(8,128)}, f32[256,256]{1,0:T(8,128)}, f32[256,256]{1,0:T(8,128)}, f32[3,256]{1,0:T(4,128)}, f32[1,256]{1,0:T(1,128)}, /*index=5*/f32[1,256]{1,0:T(1,128)}, f32[1,256]{1,0:T(1,128)}) custom-call(s32[67]{0:T(128)S(1)} %concatenate.6.place_ref, bf16[128,896]{1,0:T(8,128)(2,1)S(1)} %bitcast.30, ...), custom_call_target="tpu_custom_call" | custom-call | tf_op jit(solution)/shard_map/unpack/pallas_call | solution.py:499
  (21 shorter events, 5.3 us)
Async XLA Ops:
  0.6 0.9 %copy-start = (bf16[256,256]{1,0:T(8,128)(2,1)S(1)}, bf16[256,256]{1,0:T(8,128)(2,1)}, u32[]{:S(2)}) copy-start(bf16[256,256]{1,0:T(8,128)(2,1)} %param.14) | copy-start | bytes 393220
  3.4 6.6 %collective-permute-start = (bf16[2,4,32,256]{3,2,1,0:T(8,128)(2,1)S(1)}, bf16[2,4,32,256]{3,2,1,0:T(8,128)(2,1)S(1)}, u32[]{:S(2)}, u32[]{:S(2)}) collective-permute-start(bf16[2,4,32,256]{3,2,1,0:T(8,128)(2,1)S(1)} %get-tuple-element.65), channel_id=1, source_target_pairs={{0,1},{1,0},{2,3},{3,2},{4,5},{5,4},{6,7},{7,6},{8,9},{9,8},{10,11... | collective-permute-start | bytes 393224 | tf_op jit(solution)/shard_map/ppermute | solution.py:590
  5.6 4.5 %collective-permute-start.1 = (bf16[2,4,32,256]{3,2,1,0:T(8,128)(2,1)S(1)}, bf16[2,4,32,256]{3,2,1,0:T(8,128)(2,1)S(1)}, u32[]{:S(2)}, u32[]{:S(2)}) collective-permute-start(bf16[2,4,32,256]{3,2,1,0:T(8,128)(2,1)S(1)} %get-tuple-element.65), channel_id=1, source_target_pairs={{1,2},{2,1},{3,4},{4,3},{5,6},{6,5},{9,10},{10,9},{11,12},{12,11},... | collective-permute-start | bytes 393224 | tf_op jit(solution)/shard_map/ppermute | solution.py:590
  10.2 14.7 %copy-start.1 = (bf16[4,32,256]{2,1,0:T(8,128)(2,1)S(1)}, bf16[4,32,256]{2,1,0:T(8,128)(2,1)}, u32[]{:S(2)}) copy-start(bf16[4,32,256]{2,1,0:T(8,128)(2,1)} %param.13) | copy-start | bytes 196612
  10.2 14.7 %collective-permute-start.3 = (bf16[3,2,4,32,256]{4,3,2,1,0:T(8,128)(2,1)S(1)}, bf16[3,2,4,32,256]{4,3,2,1,0:T(8,128)(2,1)S(1)}, u32[]{:S(2)}, u32[]{:S(2)}) collective-permute-start(bf16[3,2,4,32,256]{4,3,2,1,0:T(8,128)(2,1)S(1)} %pad_maximum_fusion.here_ref), channel_id=1, source_target_pairs={{0,248},{8,16},{16,8},{24,32},{32,24},{40,48},{48,40},{56,64},{64,... | collective-permute-start | bytes 1179656 | tf_op jit(solution)/shard_map/ppermute | solution.py:590
  13.5 11.3 %collective-permute-start.2 = (bf16[3,2,4,32,256]{4,3,2,1,0:T(8,128)(2,1)S(1)}, bf16[3,2,4,32,256]{4,3,2,1,0:T(8,128)(2,1)S(1)}, u32[]{:S(2)}, u32[]{:S(2)}) collective-permute-start(bf16[3,2,4,32,256]{4,3,2,1,0:T(8,128)(2,1)S(1)} %pad_maximum_fusion.here_ref), channel_id=1, source_target_pairs={{0,8},{8,0},{16,24},{24,16},{32,40},{40,32},{48,56},{56,48},{64,72... | collective-permute-start | bytes 1179656 | tf_op jit(solution)/shard_map/ppermute | solution.py:590
  36.2 1.6 %collective-permute-start.4 = (bf16[128,896]{1,0:T(8,128)(2,1)S(1)}, bf16[128,896]{1,0:T(8,128)(2,1)S(1)}, u32[]{:S(2)}, u32[]{:S(2)}) collective-permute-start(bf16[128,896]{1,0:T(8,128)(2,1)S(1)} %get-tuple-element.46), channel_id=1, source_target_pairs={{0,8},{8,0},{1,9},{9,1},{2,10},{10,2},{3,11},{11,3},{4,12},{12,4},... | collective-permute-start | bytes 688136 | tf_op jit(solution)/shard_map/ppermute | solution.py:590
  38.6 17.0 %all-to-all-start = ((bf16[16,8,896]{2,1,0:T(8,128)(2,1)}), bf16[16,8,896]{2,1,0:T(8,128)(2,1)S(1)}, u32[]{:S(2)}, u32[]{:S(2)}) async-start(bf16[16,8,896]{2,1,0:T(8,128)(2,1)} %bitcast.17), calls=%async_computation | async-start | bytes 458752 | tf_op jit(solution)/shard_map/all_to_all | solution.py:601
  55.6 2.8 %collective-permute-start.5 = (f32[8,896]{1,0:T(8,128)S(1)}, f32[8,896]{1,0:T(8,128)S(1)}, u32[]{:S(2)}, u32[]{:S(2)}) collective-permute-start(f32[8,896]{1,0:T(8,128)S(1)} %convert_reduce_fusion), channel_id=1, source_target_pairs={{0,32},{32,0},{64,96},{96,64},{128,160},{160,128},{192,224},{224,1... | collective-permute-start | bytes 86024 | tf_op jit(solution)/shard_map/ppermute | solution.py:590
  58.4 3.6 %collective-permute-start.6 = (f32[8,896]{1,0:T(8,128)S(1)}, f32[8,896]{1,0:T(8,128)S(1)}, u32[]{:S(2)}, u32[]{:S(2)}) collective-permute-start(f32[8,896]{1,0:T(8,128)S(1)} %add.26), channel_id=1, source_target_pairs={{0,64},{32,96},{64,0},{96,32},{128,192},{160,224},{192,128},{224,1... | collective-permute-start | bytes 86024 | tf_op jit(solution)/shard_map/ppermute | solution.py:590
  62.0 4.9 %collective-permute-start.7 = (f32[8,896]{1,0:T(8,128)S(1)}, f32[8,896]{1,0:T(8,128)S(1)}, u32[]{:S(2)}, u32[]{:S(2)}) collective-permute-start(f32[8,896]{1,0:T(8,128)S(1)} %add.27), channel_id=1, source_target_pairs={{0,192},{32,224},{64,128},{96,160},{128,64},{160,96},{192,0},{224,... | collective-permute-start | bytes 86024 | tf_op jit(solution)/shard_map/ppermute | solution.py:590
  67.6 10.7 %all-to-all-start.1 = ((bf16[16,8,896]{2,1,0:T(8,128)(2,1)}), bf16[16,8,896]{2,1,0:T(8,128)(2,1)S(1)}, u32[]{:S(2)}, u32[]{:S(2)}) async-start(bf16[16,8,896]{2,1,0:T(8,128)(2,1)} %broadcast_in_dim.2), calls=%async_computation.1 | async-start | bytes 458752 | tf_op jit(solution)/shard_map/all_to_all | solution.py:601
  78.3 7.5 %collective-permute-start.8 = (bf16[128,896]{1,0:T(8,128)(2,1)S(1)}, bf16[128,896]{1,0:T(8,128)(2,1)S(1)}, u32[]{:S(2)}, u32[]{:S(2)}) collective-permute-start(bf16[128,896]{1,0:T(8,128)(2,1)S(1)} %bitcast.29), channel_id=1, source_target_pairs={{0,8},{8,0},{1,9},{9,1},{2,10},{10,2},{3,11},{11,3},{4,12},{12,4},... | collective-permute-start | bytes 688136 | tf_op jit(solution)/shard_map/ppermute | solution.py:590
